TPU v7x, 32 devices: a whole 2x2x4 slice. The times are simulated.
32 devices in a mesh: pix: 8 (over z, y), ch: 4 (over x, core).
Axes of the slice: x: 2, y: 2, z: 4, core: 2. Of those that a mesh axis runs over, the one named last changes fastest.
Arguments:
- features: bfloat16 [64, 128, 2048], P('pix', None, 'ch'), may hold values from -6 to 6
- pixel_mask: int32 [64, 128], P('pix'), may hold values from 0 to 1, as said below
- reduce_weight: bfloat16 [2048, 512], P(None, 'ch'), may hold values from -0.125 to 0.125
- reduce_gain: float32 [512], P('ch'), may hold values from 0.5 to 1.5
- reduce_bias: float32 [512], P('ch'), may hold values from -1.5 to 1.5
- dilated_weight: bfloat16 [3, 3, 512, 512], P(None, None, 'ch'), may hold values from -0.09375 to 0.09375
- dilated_gain: float32 [512], P('ch'), may hold values from 0.5 to 1.5
- dilated_bias: float32 [512], P('ch'), may hold values from -1.5 to 1.5
- expand_weight: bfloat16 [512, 2048], P('ch'), may hold values from -0.25 to 0.25
- expand_gain: float32 [2048], P('ch'), may hold values from 0.5 to 1.5
- expand_bias: float32 [2048], P('ch'), may hold values from -1.5 to 1.5
- aspp_weight: bfloat16 [3, 3, 3, 2048, 256], P(None, None, None, 'ch'), may hold values from -0.046875 to 0.046875
- aspp_gain: float32 [3, 256], P(None, 'ch'), may hold values from 0.5 to 1.5
- aspp_bias: float32 [3, 256], P(None, 'ch'), may hold values from -1.5 to 1.5
- task_weight: bfloat16 [3, 256, 23], P(None, 'ch'), may hold values from -0.21875 to 0.21875
- cotangent: float32 [64, 128, 23], P('pix'), may hold values from -24 to 24
Outputs:
- predictions: float32 [64, 128, 23], P('pix')
- features_grad: bfloat16 [64, 128, 2048], P('pix', None, 'ch')
- reduce_weight_grad: float32 [2048, 512], P('pix', 'ch')
- reduce_gain_grad: float32 [512], P('ch')
- reduce_bias_grad: float32 [512], P('ch')
- dilated_weight_grad: float32 [3, 3, 512, 512], P(None, None, 'ch', 'pix')
- dilated_gain_grad: float32 [512], P('ch')
- dilated_bias_grad: float32 [512], P('ch')
- expand_weight_grad: float32 [512, 2048], P('ch', 'pix')
- expand_gain_grad: float32 [2048], P('ch')
- expand_bias_grad: float32 [2048], P('ch')
- aspp_weight_grad: float32 [3, 3, 3, 2048, 256], P(None, None, None, 'ch', 'pix')
- aspp_gain_grad: float32 [3, 256], P(None, 'ch')
- aspp_bias_grad: float32 [3, 256], P(None, 'ch')
- task_weight_grad: float32 [3, 256, 23], P(None, 'ch')
Inputs may be any that keep to these rules, and one draw needn't show every extreme that they name: `pixel_mask`: each row holds padding; the share of image pixels rises from about 0.3 in the first rows to about 0.9 in the last.
All inputs are finite; a program needn't handle non-finite values.
Results may differ from a plain program's by a relative error of at most 0.025.
Values may be sent and summed in bfloat16 or wider, within the bound.
A program may use at most 256 MiB of HBM per device.

v0:
```python
import jax
import jax.numpy as jnp
from jax import lax
from jax.experimental import pallas as pl
from jax.experimental.pallas import tpu as pltpu
from jax.sharding import PartitionSpec as P

CLS = 19


epsilon = 1e-05
highest = lax.Precision.HIGHEST
aspp_rates = (12, 24, 36)
inner_rate = 2


def from_behind(value, axis, steps):
    count = lax.axis_size(axis)
    first, last = (max(0, -steps), min(count, count - steps))
    return lax.ppermute(value, axis, [(source, source + steps) for source in range(first, last)])


def with_halo(shard, sides, width):
    for axis, dim in sides:
        devices, length = (lax.axis_size(axis), shard.shape[dim])
        up = [(i, (i + 1) % devices) for i in range(devices - 1)]
        down = [(j, i) for i, j in up]
        last = lax.slice_in_dim(shard, length - width, length, axis=dim)
        first = lax.slice_in_dim(shard, 0, width, axis=dim)
        before = lax.ppermute(last, axis, up)
        after = lax.ppermute(first, axis, down)
        shard = jnp.concatenate([before, shard, after], axis=dim)
    return shard


def silu_slope(value):
    sigma = jax.nn.sigmoid(value)
    return sigma * (1.0 + value * (1.0 - sigma))


def shift_cols(value, offset):
    if offset == 0:
        return value
    margin = abs(offset)
    widths = [(0, 0)] * value.ndim
    widths[1] = (margin, margin)
    padded = jnp.pad(value, widths)
    return lax.slice_in_dim(padded, margin + offset, margin + offset + value.shape[1], axis=1)


def moved(piece, distance):
    return from_behind(piece, "pix", -distance)


def shift_rows(value, offset):
    if offset == 0:
        return value
    steps_over, inner = divmod(offset, value.shape[0])
    first = moved(value, steps_over)[inner:]
    if inner == 0:
        return first
    second = moved(value, steps_over + 1)[:inner]
    return jnp.concatenate([first, second], axis=0)


def halo_rows(value):
    return with_halo(value, (("pix", 0),), inner_rate)


def gather_channels(value):
    return lax.all_gather(value, "ch", axis=1, tiled=True)


def sum_channels(value):
    return lax.psum_scatter(
        value.astype(jnp.bfloat16), "ch", scatter_dimension=1, tiled=True
    ).astype(jnp.float32)


def normalized(hidden, valid, axes):
    total, count = lax.psum(
        (jnp.sum(hidden * valid, axis=axes, keepdims=True), jnp.sum(valid)), "pix"
    )
    center = total / count
    spread_sum = lax.psum(jnp.sum(valid * (hidden - center) ** 2, axis=axes, keepdims=True), "pix")
    variance = spread_sum / count
    scale = lax.rsqrt(variance + epsilon)
    return ((hidden - center) * scale, scale, count)


def norm_grad(grad_out, centered, scale, gain, count, valid, axes):
    sum_out, sum_cross = lax.psum(
        (
            jnp.sum(grad_out, axis=axes, keepdims=True),
            jnp.sum(grad_out * centered, axis=axes, keepdims=True),
        ),
        "pix",
    )
    grad_in = gain * scale * (grad_out - valid * (sum_out + centered * sum_cross) / count)
    return (grad_in, sum_cross, sum_out)


def task_scales(gram):
    norms = jnp.sqrt(jnp.diagonal(gram) + 1e-06)
    proj = gram / norms[None, :]
    vector = proj[0, 0] - proj[0, 1:]
    matrix = proj[0, 0] - proj[0, 1:][None, :] - proj[1:, 0][:, None] + proj[1:, 1:]
    determinant = matrix[0, 0] * matrix[1, 1] - matrix[0, 1] * matrix[1, 0]
    second = (vector[0] * matrix[1, 1] - vector[1] * matrix[1, 0]) / determinant
    third = (vector[1] * matrix[0, 0] - vector[0] * matrix[0, 1]) / determinant
    return jnp.stack([1.0 - second - third, second, third])


def on_device(
    features,
    pixel_mask,
    reduce_weight,
    reduce_gain,
    reduce_bias,
    dilated_weight,
    dilated_gain,
    dilated_bias,
    expand_weight,
    expand_gain,
    expand_bias,
    aspp_weight,
    aspp_gain,
    aspp_bias,
    task_weight,
    cotangent,
):
    rows_here, width, local_in = features.shape
    pixels = rows_here * width
    local_mid = reduce_weight.shape[1]
    full_mid = dilated_weight.shape[3]
    branch_width = aspp_weight.shape[4]
    outs_count = task_weight.shape[2]
    valid = pixel_mask.astype(jnp.float32).reshape(pixels, 1)
    valid_branch = valid[None]
    masked = features.reshape(pixels, local_in) * valid.astype(jnp.bfloat16)
    inputs_full = gather_channels(masked)
    hidden_one = jnp.dot(inputs_full, reduce_weight, preferred_element_type=jnp.float32)
    norm_one, scale_one, count = normalized(hidden_one, valid, (0,))
    pre_one = norm_one * reduce_gain + reduce_bias
    act_one = (jax.nn.silu(pre_one) * valid).astype(jnp.bfloat16)
    padded_one = halo_rows(act_one.reshape(rows_here, width, local_mid))
    partial_value = jnp.zeros((pixels, full_mid), jnp.float32)
    for a in range(3):
        for b in range(3):
            shifted = shift_cols(padded_one[2 * a : 2 * a + rows_here], (b - 1) * inner_rate)
            partial_value = partial_value + jnp.dot(
                shifted.reshape(pixels, local_mid),
                dilated_weight[a, b],
                preferred_element_type=jnp.float32,
            )
    hidden_two = sum_channels(partial_value)
    norm_two, scale_two, _ = normalized(hidden_two, valid, (0,))
    pre_two = norm_two * dilated_gain + dilated_bias
    act_two = (jax.nn.silu(pre_two) * valid).astype(jnp.bfloat16)
    hidden_three = sum_channels(jnp.dot(act_two, expand_weight, preferred_element_type=jnp.float32))
    norm_three, scale_three, _ = normalized(hidden_three, valid, (0,))
    pre_three = norm_three * expand_gain + expand_bias + masked.astype(jnp.float32)
    trunk_out = (
        (jax.nn.silu(pre_three) * valid).astype(jnp.bfloat16).reshape(rows_here, width, local_in)
    )
    kept_rows = []
    partials = []
    for j in range(3):
        rate = aspp_rates[j]
        running = jnp.zeros((pixels, branch_width), jnp.float32)
        shifted_rows = []
        for a in range(3):
            row_shift = shift_rows(trunk_out, (a - 1) * rate)
            shifted_rows.append(row_shift)
            for b in range(3):
                shifted = shift_cols(row_shift, (b - 1) * rate)
                running = running + jnp.dot(
                    shifted.reshape(pixels, local_in),
                    aspp_weight[j, a, b],
                    preferred_element_type=jnp.float32,
                )
        kept_rows.append(shifted_rows)
        partials.append(running)
    branch_sum = sum_channels(jnp.stack(partials).reshape(3 * pixels, branch_width)).reshape(
        3, pixels, -1
    )
    branch_gain = aspp_gain[:, None, :]
    norm_branch, scale_branch, _ = normalized(branch_sum, valid_branch, (1,))
    pre_branch = norm_branch * branch_gain + aspp_bias[:, None, :]
    branch_out = (jax.nn.silu(pre_branch) * valid_branch).astype(jnp.bfloat16)
    predictions = lax.psum(
        jnp.einsum(
            "jpc,jco->po", branch_out, task_weight, preferred_element_type=jnp.float32
        ).astype(jnp.bfloat16),
        "ch",
    ).astype(jnp.float32)
    columns = jnp.arange(outs_count)
    task_of = (columns >= CLS).astype(jnp.int32) + (columns >= CLS + 1).astype(jnp.int32)
    select = (task_of[:, None] == jnp.arange(3)[None, :]).astype(jnp.float32)
    target = cotangent.reshape(pixels, outs_count) * valid
    task_float = task_weight.astype(jnp.float32)
    task_grads = jnp.einsum("po,ot,jco->tjpc", target, select, task_float, precision=highest)
    gram = lax.psum(
        jnp.einsum("tjpc,sjpc->ts", task_grads, task_grads, precision=highest), ("pix", "ch")
    )
    scales = task_scales(gram)
    branch_grad = jnp.einsum("t,tjpc->jpc", scales, task_grads, precision=highest)
    task_weight_grad = lax.psum(
        jnp.einsum("jpc,po->jco", branch_out.astype(jnp.float32), target, precision=highest), "pix"
    )
    grad_pre_branch = branch_grad * valid_branch * silu_slope(pre_branch)
    grad_branch, aspp_gain_grad, aspp_bias_grad = norm_grad(
        grad_pre_branch, norm_branch, scale_branch, branch_gain, count, valid_branch, (1,)
    )
    grad_full = gather_channels(grad_branch.astype(jnp.bfloat16).reshape(3 * pixels, -1)).reshape(
        3, rows_here, width, -1
    )
    grad_trunk = jnp.zeros((pixels, local_in), jnp.float32)
    aspp_list = []
    for j in range(3):
        rate = aspp_rates[j]
        grad_flat = grad_full[j].reshape(pixels, -1)
        per_row = []
        for a in range(3):
            back_rows = shift_rows(grad_full[j], -(a - 1) * rate)
            per_col = []
            for b in range(3):
                shifted = shift_cols(back_rows, -(b - 1) * rate)
                grad_trunk = grad_trunk + jnp.einsum(
                    "pa,ca->pc",
                    shifted.reshape(pixels, -1),
                    aspp_weight[j, a, b],
                    preferred_element_type=jnp.float32,
                )
                forward_tap = shift_cols(kept_rows[j][a], (b - 1) * rate).reshape(pixels, local_in)
                per_col.append(
                    jnp.einsum(
                        "pc,pa->ca", forward_tap, grad_flat, preferred_element_type=jnp.float32
                    )
                )
            per_row.append(jnp.stack(per_col))
        aspp_list.append(jnp.stack(per_row))
    aspp_weight_local = jnp.stack(aspp_list)
    grad_pre_three = grad_trunk * valid * silu_slope(pre_three)
    grad_three, expand_gain_grad, expand_bias_grad = norm_grad(
        grad_pre_three, norm_three, scale_three, expand_gain, count, valid, (0,)
    )
    grad_three_full = gather_channels(grad_three.astype(jnp.bfloat16))
    grad_act_two = jnp.einsum(
        "pc,dc->pd", grad_three_full, expand_weight, preferred_element_type=jnp.float32
    )
    expand_weight_local = jnp.einsum(
        "pd,pc->dc", act_two, grad_three_full, preferred_element_type=jnp.float32
    )
    grad_pre_two = grad_act_two * valid * silu_slope(pre_two)
    grad_two, dilated_gain_grad, dilated_bias_grad = norm_grad(
        grad_pre_two, norm_two, scale_two, dilated_gain, count, valid, (0,)
    )
    grad_two_full = gather_channels(grad_two.astype(jnp.bfloat16))
    padded_grad = halo_rows(grad_two_full.reshape(rows_here, width, full_mid))
    grad_act_one = jnp.zeros((pixels, local_mid), jnp.float32)
    dilated_rows = []
    for a in range(3):
        dilated_cols = []
        for b in range(3):
            shifted = shift_cols(
                padded_grad[4 - 2 * a : 4 - 2 * a + rows_here], -(b - 1) * inner_rate
            )
            grad_act_one = grad_act_one + jnp.einsum(
                "pe,de->pd",
                shifted.reshape(pixels, full_mid),
                dilated_weight[a, b],
                preferred_element_type=jnp.float32,
            )
            forward_tap = shift_cols(
                padded_one[2 * a : 2 * a + rows_here], (b - 1) * inner_rate
            ).reshape(pixels, local_mid)
            dilated_cols.append(
                jnp.einsum(
                    "pd,pe->de", forward_tap, grad_two_full, preferred_element_type=jnp.float32
                )
            )
        dilated_rows.append(jnp.stack(dilated_cols))
    dilated_weight_local = jnp.stack(dilated_rows)
    grad_pre_one = grad_act_one * valid * silu_slope(pre_one)
    grad_one, reduce_gain_grad, reduce_bias_grad = norm_grad(
        grad_pre_one, norm_one, scale_one, reduce_gain, count, valid, (0,)
    )
    grad_one_low = grad_one.astype(jnp.bfloat16)
    input_sum = sum_channels(
        jnp.einsum("pd,cd->pc", grad_one_low, reduce_weight, preferred_element_type=jnp.float32)
    )
    features_grad = (
        ((input_sum + grad_pre_three) * valid)
        .astype(jnp.bfloat16)
        .reshape(rows_here, width, local_in)
    )
    reduce_weight_local = jnp.einsum(
        "pc,pd->cd", inputs_full, grad_one_low, preferred_element_type=jnp.float32
    )
    reduce_weight_grad, dilated_weight_grad, expand_weight_grad, aspp_weight_grad = (
        lax.psum_scatter(reduce_weight_local, "pix", scatter_dimension=0, tiled=True),
        lax.psum_scatter(dilated_weight_local, "pix", scatter_dimension=3, tiled=True),
        lax.psum_scatter(expand_weight_local, "pix", scatter_dimension=1, tiled=True),
        lax.psum_scatter(aspp_weight_local, "pix", scatter_dimension=4, tiled=True),
    )
    return (
        predictions.reshape(rows_here, width, outs_count),
        features_grad,
        reduce_weight_grad,
        reduce_gain_grad.reshape(-1),
        reduce_bias_grad.reshape(-1),
        dilated_weight_grad,
        dilated_gain_grad.reshape(-1),
        dilated_bias_grad.reshape(-1),
        expand_weight_grad,
        expand_gain_grad.reshape(-1),
        expand_bias_grad.reshape(-1),
        aspp_weight_grad,
        aspp_gain_grad.reshape(3, -1),
        aspp_bias_grad.reshape(3, -1),
        task_weight_grad,
    )


MESH = pl.DeviceIdType.MESH
ROW_CLASSES, COL_CLASSES = 2, 4
PHASES = ROW_CLASSES * COL_CLASSES
SPLIT = 4
FAR_FIRST = (6, 7, 4, 5, 2, 3, 1)
f32, bf16 = jnp.float32, jnp.bfloat16
VMEM_BYTES = 60 << 20


def shape(dims, dtype):
    return jax.ShapeDtypeStruct(dims, dtype)


def call(name, cid, kernel, arrays, outs, scratch, hbm_ins=(), hbm_outs=()):
    vmem, hbm = pl.BlockSpec(memory_space=pltpu.VMEM), pl.BlockSpec(memory_space=pl.ANY)
    return pl.pallas_call(
        kernel,
        out_shape=outs,
        in_specs=[hbm if i in hbm_ins else vmem for i in range(len(arrays))],
        out_specs=[hbm if i in hbm_outs else vmem for i in range(len(outs))],
        scratch_shapes=scratch,
        compiler_params=pltpu.CompilerParams(
            collective_id=cid, has_side_effects=True, vmem_limit_bytes=VMEM_BYTES
        ),
        name=name,
    )(*arrays)


def dma(*dims):
    return pltpu.SemaphoreType.DMA(dims)


def greet(ch, pix):
    p, c = lax.axis_index("pix"), lax.axis_index("ch")
    barrier = pltpu.get_barrier_semaphore()
    for k in ch:
        pl.semaphore_signal(barrier, inc=1, device_id=(p, c ^ k), device_id_type=MESH)
    for k in pix:
        pl.semaphore_signal(barrier, inc=1, device_id=(p ^ k, c), device_id_type=MESH)
    return barrier, len(ch) + len(pix)


def push(src, dst, send, recv, device):
    copy = pltpu.make_async_remote_copy(
        src_ref=src,
        dst_ref=dst,
        send_sem=send,
        recv_sem=recv,
        device_id=device,
        device_id_type=MESH,
    )
    copy.start()
    return copy


def keep(src, dst, sem):
    copy = pltpu.make_async_copy(src, dst, sem)
    copy.start()
    return copy


def rows(start, size):
    return pl.ds(pl.multiple_of(start, size), size)


def fold(x):
    return jnp.sum(x.reshape(x.shape[0] // 8, 8, x.shape[1]), axis=0)


def total(x):
    return jnp.sum(x, axis=0, keepdims=True)


def loop(steps, body, init):
    return lax.fori_loop(0, steps, body, init)


def sum_over_ch(part, tile, tiles, own, out, near, cross, near_sems, far_sems):
    p, c = lax.axis_index("pix"), lax.axis_index("ch")
    k, x = lax.rem(c, 2), c // 2
    n = own.shape[2]
    copies = []
    for t in range(tiles):
        at = pl.ds(t * tile, tile)
        value = part(t)
        for d in range(SPLIT):
            block = value[:, d * n : (d + 1) * n]
            own[d, at] = block
            out[d, at] = block.astype(bf16)
        copies.append(
            [
                push(
                    out.at[2 * h + 1 - k, at],
                    near.at[h, at],
                    near_sems.at[0, t, h],
                    near_sems.at[1, t, h],
                    (p, c ^ 1),
                )
                for h in range(2)
            ]
        )
    crossing = []
    for t in range(tiles):
        at = pl.ds(t * tile, tile)
        for copy in copies[t]:
            copy.wait()
        cross[0, at] = (own[2 * (1 - x) + k, at] + near[1 - x, at].astype(f32)).astype(bf16)
        crossing.append(
            push(cross.at[0, at], cross.at[1, at], far_sems.at[0, t], far_sems.at[1, t], (p, c ^ 2))
        )

    def result(t):
        at = pl.ds(t * tile, tile)
        crossing[t].wait()
        return own[2 * x + k, at] + near[x, at].astype(f32) + cross[1, at].astype(f32)

    return result


def sum_scratch(pixels, n, tiles):
    return [
        pltpu.VMEM((SPLIT, pixels, n), f32),
        pltpu.VMEM((SPLIT, pixels, n), bf16),
        pltpu.VMEM((2, pixels, n), bf16),
        pltpu.VMEM((2, pixels, n), bf16),
        dma(2, tiles, 2),
        dma(2, tiles),
    ]


def pix_exchange(send, recv, sems):
    p, c = lax.axis_index("pix"), lax.axis_index("ch")
    copies = [
        push(send, recv.at[p], sems.at[0, k], sems.at[1, k], (p ^ k, c)) for k in FAR_FIRST
    ]
    recv[p] = send[...]
    for copy in copies:
        copy.wait()


def norm_stats(hidden, valid, pixels, send, recv, sems):
    n = hidden.shape[1]
    tile = 128
    repeat = n // 128

    def mask(at):
        v = valid[at]
        return v if repeat == 1 else jnp.concatenate([v] * repeat, axis=1)

    def first(i, carry):
        at = rows(i * tile, tile)
        v = mask(at)
        return carry[0] + fold(hidden[at] * v), carry[1] + fold(v)

    zero = jnp.zeros((8, n), f32)
    sums, count = loop(pixels // tile, first, (zero, zero))
    sums, count = total(sums), total(count)
    center = sums / jnp.maximum(count, 1.0)

    def second(i, carry):
        at = rows(i * tile, tile)
        apart = hidden[at] - center
        return carry + fold(mask(at) * apart * apart)

    spread = total(loop(pixels // tile, second, zero))
    send[0:1] = sums
    send[1:2] = spread
    send[2:3] = count
    pix_exchange(send, recv, sems)
    return join(recv, PHASES)


def join(recv, parts):
    sums, count = recv[0, 0:1], recv[0, 2:3]
    for i in range(1, parts):
        sums, count = sums + recv[i, 0:1], count + recv[i, 2:3]
    center = sums / count
    spread = jnp.zeros_like(sums)
    for i in range(parts):
        n = recv[i, 2:3]
        apart = recv[i, 0:1] / jnp.maximum(n, 1.0) - center
        spread = spread + recv[i, 1:2] + n * apart * apart
    return center, lax.rsqrt(spread / count + epsilon), count


def stat_scratch(n):
    return [pltpu.VMEM((8, n), f32), pltpu.VMEM((PHASES, 8, n), f32), dma(2, PHASES)]


def silu(x):
    return x / (1.0 + jnp.exp(-x))


def gather_over_ch(full, n, tile, tiles, near_sems, far_sems, hop_sems, ready, between=None):
    p, c = lax.axis_index("pix"), lax.axis_index("ch")

    def part(owner, t):
        return full.at[pl.ds(t * tile, tile), rows(owner * n, n)]

    near, far, hops = [], [], []
    for t in range(tiles):
        ready(t)
        src = part(c, t)
        far.append(push(src, src, far_sems.at[0, t], far_sems.at[1, t], (p, c ^ 2)))
        near.append(push(src, src, near_sems.at[0, t], near_sems.at[1, t], (p, c ^ 1)))
    if between is not None:
        between()
    for t in range(tiles):
        far[t].wait_recv()
        src = part(c ^ 2, t)
        hops.append(push(src, src, hop_sems.at[0, t], hop_sems.at[1, t], (p, c ^ 1)))
    for t in range(tiles):
        far[t].wait_send()
        near[t].wait()
        hops[t].wait()


def gather_scratch(tiles):
    return [dma(2, tiles), dma(2, tiles), dma(2, tiles)]


def to_classes(x):
    rows, cols, n = x.shape
    x = x.reshape(rows // ROW_CLASSES, ROW_CLASSES, cols // COL_CLASSES, COL_CLASSES, n)
    return x.transpose(1, 3, 0, 2, 4).reshape(PHASES, -1, n)


def from_classes(x, rows, cols):
    n = x.shape[-1]
    x = x.reshape(ROW_CLASSES, COL_CLASSES, rows // ROW_CLASSES, cols // COL_CLASSES, n)
    return x.transpose(2, 0, 3, 1, 4).reshape(rows, cols, n)


RATE_ROWS = tuple(rate // ROW_CLASSES for rate in aspp_rates)
RATE_COLS = tuple(rate // COL_CLASSES for rate in aspp_rates)


def load_pyramid(weight, wide, sems):
    m = weight.shape[4]
    return [
        [keep(weight.at[j, a, b], wide.at[3 * j + a, :, b * m : (b + 1) * m], sems.at[3 * j + a, b]) for b in range(3)]
        for j in range(3)
        for a in range(3)
    ]


def move_cols(x, by):
    place = lax.broadcasted_iota(jnp.int32, x.shape, 0) % 32
    rolled = pltpu.roll(x, by % x.shape[0], 0)
    return jnp.where(place < by, 0.0, rolled) if by > 0 else jnp.where(place >= 32 + by, 0.0, rolled)


def ch_exchange(send, recv, sems):
    p, c = lax.axis_index("pix"), lax.axis_index("ch")
    copies = [push(send, recv.at[c], sems.at[0, k], sems.at[1, k], (p, c ^ k)) for k in (2, 3, 1)]
    recv[c] = send[...]
    for copy in copies:
        copy.wait()


def add_up(recv, parts):
    value = recv[0]
    for i in range(1, parts):
        value = value + recv[i]
    return value


def task_vector(square, weights):
    product = square * weights
    row = lax.broadcasted_iota(jnp.int32, (32, 32), 0)
    col = lax.broadcasted_iota(jnp.int32, (32, 32), 1)

    def task(i):
        return (i >= CLS).astype(jnp.int32) + (i >= CLS + 1).astype(jnp.int32)

    def entry(t, s):
        return jnp.sum(
            jnp.sum(jnp.where((task(row) == t) & (task(col) == s), product, 0.0), axis=1, keepdims=True),
            axis=0,
            keepdims=True,
        )

    gram = [[entry(t, s) for s in range(3)] for t in range(3)]
    norms = [jnp.sqrt(gram[k][k] + 1e-06) for k in range(3)]
    proj = [[gram[i][k] / norms[k] for k in range(3)] for i in range(3)]
    vector = [proj[0][0] - proj[0][b] for b in (1, 2)]
    matrix = [[proj[0][0] - proj[0][b] - proj[a][0] + proj[a][b] for b in (1, 2)] for a in (1, 2)]
    determinant = matrix[0][0] * matrix[1][1] - matrix[0][1] * matrix[1][0]
    second = (vector[0] * matrix[1][1] - vector[1] * matrix[1][0]) / determinant
    third = (vector[1] * matrix[0][0] - vector[0] * matrix[0][1]) / determinant
    which = task(lax.broadcasted_iota(jnp.int32, (32, 1), 0))
    return jnp.where(which == 0, 1.0 - second - third, jnp.where(which == 1, second, third))


def slope(x):
    s = 1.0 / (1.0 + jnp.exp(-x))
    return s * (1.0 + x * (1.0 - s))


def pyramid(trunk, loads, wide, moving, pass_inputs, head_copies, heads, heads_all, targets, square, *refs):
    (full, predictions, head_grad, sums, others, picks) = refs[:6]
    (sides, own, out, near, cross, hidden, grad, branch) = refs[6:14]
    (s_send, s_ch, s_mid, s_pix, b_send, b_ch, b_mid, b_pix) = refs[14:22]
    (h_send, h_ch, h_mid, h_pix, h_sum, p_send, p_ch) = refs[22:29]
    (near_sems, far_sems, ch_sems, pix_sems, g_near, g_far, g_hop, y_sems, picked, pick_sems) = refs[29:]
    p, c = lax.axis_index("pix"), lax.axis_index("ch")
    k, x = lax.rem(c, 2), c // 2
    m = wide.shape[2] // 3
    pixels, half = trunk.shape[1], trunk.shape[2]
    quarter = pixels // SPLIT
    contract0 = (((0,), (0,)), ((), ()))
    contract1 = (((1,), (1,)), ((), ()))
    mine = rows(c * quarter, quarter)
    part = pixels // SPLIT
    sharing = []

    def share(slot, quarters, own, k, first):
        for i, q in enumerate(quarters):
            at = pl.ds(q * part, part)
            src = trunk.at[:, at] if own else others.at[2 - k, :, at]
            sharing.append(
                push(src, others.at[slot, :, at], y_sems.at[0, first + i], y_sems.at[1, first + i], (p ^ k, c))
            )
        return sharing[-len(quarters) :]

    def convolve(j, h):
        s = RATE_ROWS[j] * 32
        for a in (1, 0, 2):
            if h == 0:
                for load in loads[3 * j + a]:
                    load.wait()
            w = wide[3 * j + a, h * half : (h + 1) * half]
            if a == 1:
                value = jnp.dot(trunk[h], w, preferred_element_type=f32)
                if h == 0:
                    sides[j] = value
                else:
                    sides[j] += value
            elif a == 0:
                sides[j, s:] += jnp.dot(trunk[h, : pixels - s], w, preferred_element_type=f32)
            else:
                sides[j, : pixels - s] += jnp.dot(trunk[h, s:], w, preferred_element_type=f32)

    for copy in moving[0]:
        copy.wait()
    for j in range(3):
        convolve(j, 0)
    inputs_done = pass_inputs()
    for copy in moving[1]:
        copy.wait()
    from_y = share(0, (0, 1), True, 1, 0)
    from_z = share(1, (2, 3), True, 2, 2)

    def pass_on(i):
        from_y[i].wait_recv()
        share(2, (i,), False, 2, 4 + i)
        from_z[i].wait_recv()
        share(2, (i + 2,), False, 1, 6 + i)

    copies = []
    for j in range(3):
        q = RATE_COLS[j]
        convolve(j, 1)
        if j == 2:
            pass_on(0)
        for d in range(SPLIT):
            at = slice(d * quarter, (d + 1) * quarter)
            value = (
                sides[j, at, m : 2 * m]
                + move_cols(sides[j, at, :m], q)
                + move_cols(sides[j, at, 2 * m :], -q)
            )
            own[d, j] = value
            out[d, j] = value.astype(bf16)
        copies.append(
            [
                push(out.at[2 * h + 1 - k, j], near.at[h, j], near_sems.at[0, j, h], near_sems.at[1, j, h], (p, c ^ 1))
                for h in range(2)
            ]
        )
        if j > 0:
            copies[j - 1] = cross_chips(copies[j - 1], j - 1, own, near, cross, far_sems)
    copies[2] = cross_chips(copies[2], 2, own, near, cross, far_sems)
    for copy in head_copies:
        copy.wait()
    each = m // SPLIT
    for j in range(3):
        for d in range(SPLIT):
            heads[:, (j * SPLIT + d) * each : (j * SPLIT + d + 1) * each] = heads_all[d, :, j * each : (j + 1) * each]
    gain, bias = heads[32:33], heads[33:34]
    head = heads[:32]
    scaled = head * task_vector(
        add_up(square, PHASES)[:, :32], lax.dot_general(head, head, contract1, precision=highest)
    )
    target = jnp.concatenate([targets[2 * c], targets[2 * c + 1]], axis=1)
    mask = lax.dot_general(
        target[24:].astype(bf16), jnp.ones((8, m), bf16), contract0, preferred_element_type=f32
    )
    grad[...] = lax.dot_general(target, scaled, contract0, precision=highest) * jnp.concatenate([mask] * 3, axis=1)
    pass_on(1)
    count = total(mask)
    for j in range(3):
        copies[j].wait()
        value = own[2 * x + k, j] + near[x, j].astype(f32) + cross[1, j].astype(f32)
        at = slice(j * m, (j + 1) * m)
        hidden[:, at] = value
        first = total(value * mask)
        apart = value - first / jnp.maximum(count, 1.0)
        s_send[j : j + 1] = first
        s_send[3 + j : 4 + j] = total(apart * apart * mask)
    s_send[6:7] = count
    s_send[7:8] = jnp.zeros((1, m), f32)

    def merge(recv, parts):
        number = recv[0, 6:7]
        for i in range(1, parts):
            number = number + recv[i, 6:7]
        whole, spread = recv[0, 0:3], recv[0, 3:6]
        for i in range(1, parts):
            whole, spread = whole + recv[i, 0:3], spread + recv[i, 3:6]
        center = whole / jnp.maximum(number, 1.0)
        for i in range(parts):
            n = recv[i, 6:7]
            apart = recv[i, 0:3] / jnp.maximum(n, 1.0) - center
            spread = spread + n * apart * apart
        return whole, spread, number

    ch_exchange(s_send, s_ch, ch_sems.at[0])
    whole, spread, number = merge(s_ch, SPLIT)
    s_mid[0:3] = whole
    s_mid[3:6] = spread
    s_mid[6:7] = number
    s_mid[7:8] = jnp.zeros((1, m), f32)
    pix_exchange(s_mid, s_pix, pix_sems.at[0])
    share(0, (2,), True, 1, 8)
    share(1, (0,), True, 2, 9)
    whole, spread, number = merge(s_pix, PHASES)
    center, scale = whole / number, lax.rsqrt(spread / number + epsilon)
    for j in range(3):
        at = slice(j * m, (j + 1) * m)
        norm = (hidden[:, at] - center[j : j + 1]) * scale[j : j + 1]
        hidden[:, at] = norm
        value = norm * gain[:, at] + bias[:, at]
        branch[:, at] = (silu(value) * mask).astype(bf16)
        back = grad[:, at] * slope(value)
        grad[:, at] = back
        b_send[j : j + 1] = total(back)
        b_send[3 + j : 4 + j] = total(back * norm)
    b_send[6:8] = jnp.zeros((2, m), f32)
    to_ch = [push(b_send, b_ch.at[c], ch_sems.at[3, 0, i], ch_sems.at[3, 1, i], (p, c ^ i)) for i in (2, 3, 1)]
    b_ch[c] = b_send[...]
    high = target.astype(bf16)
    rest = target - high.astype(f32)
    middle = rest.astype(bf16)
    low = (rest - middle.astype(f32)).astype(bf16)
    p_send[...] = lax.dot_general(
        head.astype(bf16), branch[...], contract1, preferred_element_type=f32
    )
    value = jnp.dot(jnp.concatenate([high, middle, low]), branch[...], preferred_element_type=f32)
    h_send[...] = value[:32] + (value[32:64] + value[64:])
    background = [push(p_send, p_ch.at[c], ch_sems.at[1, 0, i], ch_sems.at[1, 1, i], (p, c ^ i)) for i in (2, 3, 1)] + [
        push(h_send.at[rows((c ^ i) * 8, 8)], h_ch.at[c], ch_sems.at[2, 0, i], ch_sems.at[2, 1, i], (p, c ^ i))
        for i in (2, 3, 1)
    ]
    p_ch[c] = p_send[...]
    h_ch[c] = h_send[rows(c * 8, 8)]
    for copy in to_ch:
        copy.wait()
    b_mid[...] = add_up(b_ch, SPLIT)
    sending = [
        push(b_mid, b_pix.at[p], pix_sems.at[1, 0, i], pix_sems.at[1, 1, i], (p ^ i, c)) for i in FAR_FIRST
    ]
    b_pix[p] = b_mid[...]
    for copy in background:
        copy.wait()
    h_mid[...] = add_up(h_ch, SPLIT)

    def block(to):
        return p_ch.at[to // 2, :, rows(lax.rem(to, 2) * 128, 128)]

    background = [
        push(block(p ^ i), predictions.at[p], pix_sems.at[2, 0, i], pix_sems.at[2, 1, i], (p ^ i, c)) for i in FAR_FIRST
    ] + [push(h_mid, h_pix.at[p], pix_sems.at[3, 0, i], pix_sems.at[3, 1, i], (p ^ i, c)) for i in FAR_FIRST]
    predictions[p] = block(p)[...]
    h_pix[p] = h_mid[...]
    for copy in sending:
        copy.wait()
    summed = add_up(b_pix, PHASES)
    sums[...] = summed
    for j in range(3):
        at = slice(j * m, (j + 1) * m)
        value = grad[:, at] - mask * (summed[j : j + 1] + hidden[:, at] * summed[3 + j : 4 + j]) / number
        full[mine, at] = (gain[:, at] * scale[j : j + 1] * value).astype(bf16)
    far = push(full.at[mine], full.at[mine], g_far.at[0], g_far.at[1], (p, c ^ 2))
    by = push(full.at[mine], full.at[mine], g_near.at[0], g_near.at[1], (p, c ^ 1))
    group = lax.rem(p, 4)
    pick = pick_rows(m, m, 0)
    for j in range(3):
        value = lax.dot_general(
            pick, full[mine, j * m : (j + 1) * m], contract1, preferred_element_type=f32
        ).astype(bf16)
        for g in range(4):
            picked[g, j * 64 : (j + 1) * 64] = value[g * 64 : (g + 1) * 64]
    sent_picks = [
        push(picked.at[group ^ i], picks.at[i - 1], pick_sems.at[0, i], pick_sems.at[1, i], (p ^ i, c)) for i in (3, 1, 2)
    ]
    for copy in background:
        copy.wait()
    own_rows = add_up(h_pix, PHASES)
    h_sum[...] = own_rows
    head_grad[rows(c * 8, 8)] = own_rows
    last = [
        push(h_sum, head_grad.at[rows(c * 8, 8)], ch_sems.at[4, 0, i], ch_sems.at[4, 1, i], (p, c ^ i))
        for i in (2, 3, 1)
    ]
    far.wait_recv()
    theirs = rows((c ^ 2) * quarter, quarter)
    hop = push(full.at[theirs], full.at[theirs], g_hop.at[0], g_hop.at[1], (p, c ^ 1))
    far.wait_send()
    by.wait()
    hop.wait()
    for copy in last:
        copy.wait()
    for copy in from_y + from_z:
        copy.wait_send()
    for copy in sharing[4:] + sent_picks:
        copy.wait()
    inputs_done()


def pick_rows(m, count, first):
    row = lax.broadcasted_iota(jnp.int32, (count, m), 0)
    col = lax.broadcasted_iota(jnp.int32, (count, m), 1)
    source = (4 * (row % 64 // 32) + row // 64 + first) * 32 + row % 32
    return jnp.where(col == source, 1.0, 0.0).astype(bf16)


def cross_chips(near_copies, j, own, near, cross, sems):
    p, c = lax.axis_index("pix"), lax.axis_index("ch")
    k, x = lax.rem(c, 2), c // 2
    for copy in near_copies:
        copy.wait()
    cross[0, j] = (own[2 * (1 - x) + k, j] + near[1 - x, j].astype(f32)).astype(bf16)
    return push(cross.at[0, j], cross.at[1, j], sems.at[0, j], sems.at[1, j], (p, c ^ 2))


def pyramid_scratch(pixels, n, m):
    quarter = pixels // SPLIT
    small = [
        pltpu.VMEM((8, m), f32),
        pltpu.VMEM((SPLIT, 8, m), f32),
        pltpu.VMEM((8, m), f32),
        pltpu.VMEM((PHASES, 8, m), f32),
    ]
    return [
        pltpu.VMEM((3, pixels, 3 * m), f32),
        pltpu.VMEM((SPLIT, 3, quarter, m), f32),
        pltpu.VMEM((SPLIT, 3, quarter, m), bf16),
        pltpu.VMEM((2, 3, quarter, m), bf16),
        pltpu.VMEM((2, 3, quarter, m), bf16),
        pltpu.VMEM((quarter, 3 * m), f32),
        pltpu.VMEM((quarter, 3 * m), f32),
        pltpu.VMEM((quarter, 3 * m), bf16),
        *small,
        *small,
        pltpu.VMEM((32, 3 * m), f32),
        pltpu.VMEM((SPLIT, 8, 3 * m), f32),
        pltpu.VMEM((8, 3 * m), f32),
        pltpu.VMEM((PHASES, 8, 3 * m), f32),
        pltpu.VMEM((8, 3 * m), f32),
        pltpu.VMEM((32, quarter), f32),
        pltpu.VMEM((SPLIT, 32, quarter), f32),
        dma(2, 3, 2),
        dma(2, 3),
        dma(5, 2, SPLIT),
        dma(4, 2, PHASES),
        dma(2),
        dma(2),
        dma(2),
        dma(2, 10),
        pltpu.VMEM((4, 192, quarter), bf16),
        dma(2, 4),
    ]


TILES = 4


def one_hot(rows_count, cols_count, source):
    row = lax.broadcasted_iota(jnp.int32, (rows_count, cols_count), 0)
    col = lax.broadcasted_iota(jnp.int32, (rows_count, cols_count), 1)
    return col == source(row)


def stage_one(feat, mask, weight, expand, gain, bias, *refs):
    (masked, reduce_rows, expand_cols, norm, padded, stat, valid) = refs[:7]
    (wide, hidden, own, out, near, cross, near_sems, far_sems, send, recv, stat_sems) = refs[7:18]
    (weight_sems, local_sems, halo_sems) = refs[18:]
    p, c = lax.axis_index("pix"), lax.axis_index("ch")
    pixels, local_in = feat.shape
    local_mid = weight.shape[1]
    tile = pixels // TILES

    def piece(i, to):
        return (
            (weight.at[rows(to * local_in, local_in), :], reduce_rows.at[:, rows(c * local_mid, local_mid)]),
            (expand.at[:, rows(to * local_in, local_in)], expand_cols.at[rows(c * local_mid, local_mid), :]),
        )[i]

    def to_ch(i):
        return [
            push(*piece(i, c ^ k), weight_sems.at[0, k, i], weight_sems.at[1, k, i], (p, c ^ k)) for k in (2, 3, 1)
        ] + [keep(*piece(i, c), local_sems.at[i])]

    reduce_copies = to_ch(0)

    present = mask[...].astype(f32)
    order = one_hot(128, 128, lambda i: 4 * (i % 32) + i // 32)
    ones = jnp.ones((128, 128), bf16)
    for r in range(8):
        column = jnp.dot(
            jnp.where(order, present[r : r + 1], 0.0).astype(bf16), ones, preferred_element_type=f32
        )
        for b in range(COL_CLASSES):
            block = ((r % ROW_CLASSES) * COL_CLASSES + b) * 128 + (r // ROW_CLASSES) * 32
            valid[block : block + 32] = column[b * 32 : (b + 1) * 32]
    for r in range(8):
        for g in range(local_in // 128):
            lanes = slice(g * 128, (g + 1) * 128)
            wide[g] = feat[r * 128 : (r + 1) * 128, lanes].astype(f32)
            for b in range(COL_CLASSES):
                block = ((r % ROW_CLASSES) * COL_CLASSES + b) * 128 + (r // ROW_CLASSES) * 32
                value = wide[g, pl.ds(b, 32, stride=COL_CLASSES), :] * valid[block : block + 32]
                masked[block : block + 32, lanes] = value.astype(bf16)

    for copy in reduce_copies:
        copy.wait()

    def part(t):
        return jnp.dot(masked[t * tile : (t + 1) * tile], reduce_rows[...], preferred_element_type=f32)

    result = sum_over_ch(part, tile, TILES, own, out, near, cross, near_sems, far_sems)
    for t in range(TILES):
        hidden[t * tile : (t + 1) * tile] = result(t)
    later = to_ch(1)
    center, scale, count = norm_stats(hidden, valid, pixels, send, recv, stat_sems)
    stat[0:1] = center
    stat[1:2] = scale
    stat[2:3] = count
    for i in range(PHASES):
        at = pl.ds(i * 128, 128)
        value = (hidden[at] - center) * scale
        norm[at] = value
        act = silu(value * gain[...] + bias[...]) * valid[at]
        padded[i, 1:5] = act.astype(bf16).reshape(4, 32, local_mid)
    up = lambda: pltpu.make_async_remote_copy(
        src_ref=padded.at[:, 4],
        dst_ref=padded.at[:, 0],
        send_sem=halo_sems.at[0, 0],
        recv_sem=halo_sems.at[1, 0],
        device_id=(p + 1, c),
        device_id_type=MESH,
    )
    down = lambda: pltpu.make_async_remote_copy(
        src_ref=padded.at[:, 1],
        dst_ref=padded.at[:, 5],
        send_sem=halo_sems.at[0, 1],
        recv_sem=halo_sems.at[1, 1],
        device_id=(p - 1, c),
        device_id_type=MESH,
    )
    first, last = p == 0, p == PHASES - 1

    @pl.when(jnp.logical_not(last))
    def _():
        up().start()

    @pl.when(jnp.logical_not(first))
    def _():
        down().start()

    @pl.when(last)
    def _():
        padded[:, 5] = jnp.zeros((PHASES, 32, local_mid), bf16)

    @pl.when(first)
    def _():
        padded[:, 0] = jnp.zeros((PHASES, 32, local_mid), bf16)

    @pl.when(jnp.logical_not(last))
    def _():
        up().wait_send()
        down().wait_recv()

    @pl.when(jnp.logical_not(first))
    def _():
        down().wait_send()
        up().wait_recv()

    return later


def prepare_heads(mask, head_weight, head_gain, head_bias, cotangent, *refs):
    (heads_all, targets_all, square_all, heads, targets, square, image, head_sems, pix_sems, local_sems) = refs
    p, c = lax.axis_index("pix"), lax.axis_index("ch")
    contract1 = (((1,), (1,)), ((), ()))
    present = mask[...].astype(f32)
    columns, m = head_weight.shape[1], head_weight.shape[2]
    heads[...] = jnp.zeros(heads.shape, f32)
    for j in range(3):
        heads[:columns, j * m : (j + 1) * m] = head_weight[j].astype(f32)
        heads[32:33, j * m : (j + 1) * m] = head_gain[j : j + 1]
        heads[33:34, j * m : (j + 1) * m] = head_bias[j : j + 1]

    image[...] = jnp.zeros(image.shape, f32)
    for r in range(8):
        at = slice(r * 128, (r + 1) * 128)
        image[:columns, at] = cotangent[:, at] * present[r : r + 1]
        image[31:32, at] = present[r : r + 1]
    square[...] = jnp.zeros(square.shape, f32)
    square[:, :32] = lax.dot_general(
        image[...], image[...], contract1, precision=highest, preferred_element_type=f32
    )
    place = jnp.where(
        one_hot(512, 512, lambda i: i % 4 * 128 + i // 128 * 32 + i % 128 // 4), 1.0, 0.0
    )
    for a in range(ROW_CLASSES):
        some = jnp.concatenate([image[:, (2 * r + a) * 128 : (2 * r + a + 1) * 128] for r in range(4)], axis=1)
        value = jnp.dot(some, place, precision=highest, preferred_element_type=f32)
        for b in range(COL_CLASSES):
            targets[a * COL_CLASSES + b] = value[:, b * 128 : (b + 1) * 128]
    copies = [push(heads, heads_all.at[c], head_sems.at[0, k], head_sems.at[1, k], (p, c ^ k)) for k in (2, 3, 1)]
    copies += [
        push(targets.at[p ^ k], targets_all.at[p], pix_sems.at[0, k, 0], pix_sems.at[1, k, 0], (p ^ k, c))
        for k in FAR_FIRST
    ] + [push(square, square_all.at[p], pix_sems.at[0, k, 1], pix_sems.at[1, k, 1], (p ^ k, c)) for k in FAR_FIRST]
    copies.append(keep(heads, heads_all.at[c], local_sems.at[0]))
    copies.append(keep(targets.at[p], targets_all.at[p], local_sems.at[1]))
    copies.append(keep(square, square_all.at[p], local_sems.at[2]))
    return copies


def stage_two(padded, valid, weight, gain, bias, *refs):
    (norm, full, taps, stat) = refs[:4]
    (hidden, own, out, near, cross, near_sems, far_sems, send, recv, stat_sems) = refs[4:14]
    (g_near, g_far, g_hop) = refs[14:]
    p, c = lax.axis_index("pix"), lax.axis_index("ch")
    pixels = valid.shape[0]
    local_mid = padded.shape[3]
    tile = pixels // TILES
    place = lax.broadcasted_iota(jnp.int32, (192, local_mid), 0) % 32
    for i in range(PHASES):
        beta = i % COL_CLASSES
        plain = padded[i].reshape(192, local_mid)
        wide = plain.astype(f32)
        if beta >= 2:
            moved_by = jnp.where(place == 0, 0.0, pltpu.roll(wide, 1, 0)).astype(bf16)
        else:
            moved_by = jnp.where(place == 31, 0.0, pltpu.roll(wide, 191, 0)).astype(bf16)
        for a in range(3):
            at = slice(a * 32, a * 32 + 128)
            for b, other, value in (
                (1, beta, plain),
                (0, (beta + 2) % 4, moved_by if beta >= 2 else plain),
                (2, (beta + 2) % 4, plain if beta >= 2 else moved_by),
            ):
                to = (i - beta + other) * 128
                col = (a * 3 + b) * local_mid
                taps[to : to + 128, col : col + local_mid] = value[at]

    def part(t):
        return jnp.dot(taps[t * tile : (t + 1) * tile], weight[...], preferred_element_type=f32)

    result = sum_over_ch(part, tile, TILES, own, out, near, cross, near_sems, far_sems)
    for t in range(TILES):
        hidden[t * tile : (t + 1) * tile] = result(t)
    center, scale, count = norm_stats(hidden, valid, pixels, send, recv, stat_sems)
    stat[0:1] = center
    stat[1:2] = scale
    stat[2:3] = count

    def ready(t):
        for i in range(tile // 128):
            at = pl.ds(t * tile + i * 128, 128)
            value = (hidden[at] - center) * scale
            norm[at] = value
            act = silu(value * gain[...] + bias[...]) * valid[at]
            full[at, rows(c * local_mid, local_mid)] = act.astype(bf16)

    gather_over_ch(full, local_mid, tile, TILES, g_near, g_far, g_hop, ready)


def stage_three(full, weight, masked, valid, gain, bias, *refs):
    (norm, classes, stat, inputs) = refs[:4]
    (hidden, trunk, send, recv, stat_sems, class_sems, own_sem, in_sems) = refs[4:]
    p, c = lax.axis_index("pix"), lax.axis_index("ch")
    pixels, n = masked.shape
    tile = pixels // TILES
    for t in range(TILES):
        at = pl.ds(t * tile, tile)
        hidden[at] = jnp.dot(full[at], weight[...], preferred_element_type=f32)
    far = push(masked, inputs.at[c], in_sems.at[0, 0], in_sems.at[1, 0], (p, c ^ 2))
    near = push(masked, inputs.at[c], in_sems.at[0, 1], in_sems.at[1, 1], (p, c ^ 1))
    mine = keep(masked, inputs.at[c], own_sem.at[2])
    center, scale, count = norm_stats(hidden, valid, pixels, send, recv, stat_sems)
    stat[0:1] = center
    stat[1:2] = scale
    stat[2:3] = count

    half = n // 2

    def finish(to, h):
        lanes = slice(h * half, (h + 1) * half)

        def step(i, carry):
            at = rows(to * 128 + i * 64, 64)
            value = (hidden[at, lanes] - center[:, lanes]) * scale[:, lanes]
            norm[at, lanes] = value
            pre = value * gain[:, lanes] + bias[:, lanes] + masked[at, lanes].astype(f32)
            v = valid[at]
            trunk[h, at] = (silu(pre) * jnp.concatenate([v] * (half // 128), axis=1)).astype(bf16)
            return carry

        loop(2, step, 0)

    copies = []
    for h in range(2):
        some = []
        for k in FAR_FIRST:
            to = p ^ k
            finish(to, h)
            some.append(
                push(
                    trunk.at[h, rows(to * 128, 128)],
                    classes.at[h, rows(p * 128, 128)],
                    class_sems.at[0, h, k],
                    class_sems.at[1, h, k],
                    (to, c),
                )
            )
        finish(p, h)
        some.append(keep(trunk.at[h, rows(p * 128, 128)], classes.at[h, rows(p * 128, 128)], own_sem.at[h]))
        copies.append(some)

    def pass_inputs():
        far.wait_recv()
        hop = push(inputs.at[c ^ 2], inputs.at[c ^ 2], in_sems.at[0, 2], in_sems.at[1, 2], (p, c ^ 1))

        def done():
            far.wait_send()
            near.wait()
            mine.wait()
            hop.wait()

        return done

    return copies, pass_inputs


def forward(
    feat, mask, weight, expand, gain1, bias1, head_weight, head_gain, head_bias, cotangent, dilated, gain2, bias2,
    gain3, bias3, pyramid_weight, *refs
):
    saved, stats, (inputs, grads, predictions, head_grad, branch_sums, others, picks) = refs[:10], refs[10:13], refs[13:20]
    padded, wide, w_sems, heads_full, save_sems = refs[20:25]
    masked, reduce_rows, expand_cols, norm1, valid, norm2, full2, taps, norm3, classes = refs[25:35]
    stat1, stat2, stat3 = stats
    own = refs[35:]
    saving = []

    def save(*which):
        for i in which:
            saving.append(keep(refs[25 + i], saved[i], save_sems.at[i]))

    one, two, three, heads = 14, 13, 8, 10
    barrier, expected = greet((1, 2, 3), FAR_FIRST)
    loads = load_pyramid(pyramid_weight, wide, w_sems)
    pl.semaphore_wait(barrier, expected)
    expand_copies = stage_one(
        feat, mask, weight, expand, gain1, bias1, masked, reduce_rows, expand_cols, norm1, padded, stat1, valid, *own[:one]
    )
    own = own[one:]
    save(0, 1, 3, 4)
    stage_two(padded, valid, dilated, gain2, bias2, norm2, full2, taps, stat2, *own[:two])
    own = own[two:]
    for copy in expand_copies:
        copy.wait()
    save(2, 5, 6, 7)
    moving, pass_inputs = stage_three(
        full2, expand_cols, masked, valid, gain3, bias3, norm3, classes, stat3, inputs, *own[:three]
    )
    own = own[three:]
    save(8)
    head_copies = prepare_heads(mask, head_weight, head_gain, head_bias, cotangent, *own[:heads])
    pyramid(
        classes, loads, wide, moving, pass_inputs, head_copies, heads_full, *own[:3],
        grads, predictions, head_grad, branch_sums, others, picks, *own[heads:],
    )
    save(9)
    for copy in saving:
        copy.wait()


def run_forward(
    cid, feat, mask, weight, expand, gain1, bias1, head_weight, head_gain, head_bias, cotangent, dilated, gain2, bias2,
    gain3, bias3, pyramid_weight
):
    pixels, n = feat.shape
    mid = weight.shape[1]
    all_mid = SPLIT * mid
    m = pyramid_weight.shape[4]
    quarter = pixels // SPLIT
    saved = [
        ((pixels, n), bf16),
        ((n, all_mid), bf16),
        ((all_mid, n), bf16),
        ((pixels, mid), f32),
        ((pixels, 128), f32),
        ((pixels, mid), f32),
        ((pixels, all_mid), bf16),
        ((pixels, 9 * mid), bf16),
        ((pixels, n), f32),
        ((2, pixels, n // 2), bf16),
    ]
    outs = [shape(*each) for each in saved] + [
        shape((8, mid), f32),
        shape((8, mid), f32),
        shape((8, n), f32),
        shape((SPLIT, pixels, n), bf16),
        shape((pixels, 3 * m), bf16),
        shape((PHASES, 32, 128), f32),
        shape((32, 3 * m), f32),
        shape((8, m), f32),
        shape((3, 2, pixels, n // 2), bf16),
        shape((3, 192, quarter), bf16),
    ]
    scratch = [
        pltpu.VMEM((PHASES, 6, 32, mid), bf16),
        pltpu.VMEM((9, n, 3 * m), bf16),
        dma(9, 3),
        pltpu.VMEM((40, 3 * m), f32),
        dma(10),
        *[pltpu.VMEM(*each) for each in saved],
        pltpu.VMEM((n // 128, 128, 128), f32),
        pltpu.VMEM((pixels, mid), f32),
        *sum_scratch(pixels, mid, TILES),
        *stat_scratch(mid),
        dma(2, SPLIT, 2),
        dma(2),
        dma(2, 2),
        pltpu.VMEM((pixels, mid), f32),
        *sum_scratch(pixels, mid, TILES),
        *stat_scratch(mid),
        *gather_scratch(TILES),
        pltpu.VMEM((pixels, n), f32),
        pltpu.VMEM((2, pixels, n // 2), bf16),
        *stat_scratch(n),
        dma(2, 2, PHASES),
        dma(4),
        dma(2, 3),
        pltpu.VMEM((SPLIT, 40, 256), f32),
        pltpu.VMEM((PHASES, 32, 128), f32),
        pltpu.VMEM((PHASES, 32, 128), f32),
        pltpu.VMEM((40, 256), f32),
        pltpu.VMEM((PHASES, 32, 128), f32),
        pltpu.VMEM((32, 128), f32),
        pltpu.VMEM((32, pixels), f32),
        dma(2, SPLIT),
        dma(2, PHASES, 2),
        dma(3),
        *pyramid_scratch(pixels, n, m),
    ]
    arrays = [
        feat, mask, weight, expand, gain1, bias1, head_weight, head_gain, head_bias, cotangent, dilated, gain2, bias2,
        gain3, bias3, pyramid_weight,
    ]
    return call("forward", cid, forward, arrays, outs, scratch, hbm_ins=(15,), hbm_outs=(*range(10), 13, 18))


PACE = (1, 10, 18, 21)


def packed_sums(values, send):
    i = 0
    for value in values:
        for g in range(value.shape[1] // 128):
            send[i : i + 1] = value[:, g * 128 : (g + 1) * 128]
            i += 1


def unpacked_sums(recv, rows_each, count):
    out, i = [], 0
    for _ in range(count):
        parts = []
        for _ in range(rows_each):
            value = recv[0, i : i + 1]
            for d in range(1, PHASES):
                value = value + recv[d, i : i + 1]
            parts.append(value)
            i += 1
        out.append(parts[0] if rows_each == 1 else jnp.concatenate(parts, axis=1))
    return out


def spread_lanes(v, n):
    return v if n == 128 else jnp.concatenate([v] * (n // 128), axis=1)


def backward(
    grads, trunk, others, weight, norm3, masked, valid, expand, gain3, bias3, norm2, gain2, bias2, full2, taps, dilated,
    norm1, gain1, bias1, reduce_rows, stats1, stats2, stats3, picks, inputs, *refs
):
    stored = (valid, norm3, masked, expand, norm2, full2, norm1, dilated, reduce_rows)
    valid, norm3, masked, expand, norm2, full2, norm1, dilated, reduce_rows, store_sems = refs[-10:]
    refs = refs[:-10]
    outs, scratch = refs[:6], refs[6:]
    (features_grad, aspp_parts, dilated_grad, expand_grad, reduce_grad, sums_out) = outs
    (wide, moved, acc, dsend, drecv, tpad, r_in, picked_in, turned, zsend, r_y) = scratch[:11]
    (gp3, g3, own, out, near, cross, hidden, gp2, g2, prod, edges, g1) = scratch[11:23]
    gp1, lanes = gp2, own
    (st3, st3r, st2, st2r, st1, st1r, e_part, e_mid, e_in, e_y, e_sum, d_part, d_in, d_y, d_sum, r_mid, r_sum) = scratch[23:40]
    (w_sems, d_sems, y_sems, z_sems, near_sems, far_sems, st_sems, gn, gf, gh, gn1, gf1, gh1, edge_sems, ch_sems, pix_sems, pair_sems, own_sems, tap_sems, in_sems, fill_sems, last_sems, slope1, d_near, d_far, mid_sems) = scratch[40:]
    p, c = lax.axis_index("pix"), lax.axis_index("ch")
    y, z = lax.rem(p, 2), p // 2
    lower = lax.rem(z, 2)
    pixels, n = norm3.shape
    m = weight.shape[4]
    mid = norm2.shape[1]
    tile = pixels // TILES
    contract0 = (((0,), (0,)), ((), ()))
    contract1 = (((1,), (1,)), ((), ()))
    count = stats1[2:3, :1]
    barrier, expected = greet((1, 2, 3), FAR_FIRST)
    loads = load_pyramid(weight, wide, w_sems)
    arrived = dict(
        zip(
            ("valid", "norm3", "masked", "expand", "norm2", "full2", "norm1", "dilated", "reduce"),
            [keep(a, b, store_sems.at[i]) for i, (a, b) in enumerate(
                zip(stored, (valid, norm3, masked, expand, norm2, full2, norm1, dilated, reduce_rows))
            )],
        )
    )

    group, upper = lax.rem(p, 4), p // 4
    quarter = picks.shape[2]
    pl.semaphore_wait(barrier, expected)
    mine = rows(c * quarter, quarter)
    sent_picks = [
        push(picks, picked_in.at[:, :, mine], y_sems.at[0, k], y_sems.at[1, k], (p, c ^ k)) for k in (2, 3, 1)
    ] + [keep(picks, picked_in.at[:, :, mine], y_sems.at[0, 0])]
    part = pixels // SPLIT
    filled = []
    for k in range(4):
        for h in range(2):
            cols = slice(h * m, (h + 1) * m)
            source = (others.at[k - 1] if k else trunk).at[h]
            here = {0: ((0, 4),), 1: ((0, 3),), 2: ((0, 1), (2, 4)), 3: ((0, 4),)}[k]
            for i, (first, end) in enumerate(here):
                at = pl.ds(first * part, (end - first) * part)
                filled.append(
                    keep(source.at[at], tpad.at[k, pl.ds(64 + first * part, (end - first) * part), cols], fill_sems.at[k, h, i])
                )
            if k in (1, 2):
                q = 3 if k == 1 else 1
                filled.append(
                    push(
                        trunk.at[h, pl.ds(q * part, part)],
                        tpad.at[k, pl.ds(64 + q * part, part), cols],
                        last_sems.at[0, k - 1, h],
                        last_sems.at[1, k - 1, h],
                        (p ^ k, c),
                    )
                )
    for i in range(4):
        tpad[i, :64] = jnp.zeros((64, n), bf16)
        tpad[i, 64 + pixels :] = jnp.zeros((64, n), bf16)

    for j in range(3):
        q = RATE_COLS[j]
        plain = grads[:, j * m : (j + 1) * m]
        value = plain.astype(f32)
        moved[j, :, :m] = move_cols(value, -q).astype(bf16)
        moved[j, :, m : 2 * m] = plain
        moved[j, :, 2 * m :] = move_cols(value, q).astype(bf16)
    back = []
    for h in range(2):
        half = slice(h * m, (h + 1) * m)
        for j in range(3):
            s = RATE_ROWS[j] * 32
            for a in (1, 0, 2):
                if h == 0:
                    for load in loads[3 * j + a]:
                        load.wait()
                w = wide[3 * j + a, half]
                if a == 1:
                    value = lax.dot_general(moved[j], w, contract1, preferred_element_type=f32)
                    if j == 0:
                        acc[...] = value
                    else:
                        acc[...] += value
                elif a == 0:
                    acc[: pixels - s] += lax.dot_general(moved[j, s:], w, contract1, preferred_element_type=f32)
                else:
                    acc[s:] += lax.dot_general(moved[j, : pixels - s], w, contract1, preferred_element_type=f32)
        dsend[h] = acc[...].astype(bf16)
        for k in FAR_FIRST:
            back.append(
                push(
                    dsend.at[h, rows((p ^ k) * 128, 128)],
                    drecv.at[h, rows(p * 128, 128)],
                    d_sems.at[0, h, k],
                    d_sems.at[1, h, k],
                    (p ^ k, c),
                )
            )
        back.append(keep(dsend.at[h, rows(p * 128, 128)], drecv.at[h, rows(p * 128, 128)], own_sems.at[h]))

    all_inputs = [
        keep(inputs.at[i // 2, pl.ds(i % 2 * n, n)], wide.at[i, :, :n], in_sems.at[i]) for i in range(8)
    ]
    cut = moved.shape[2]
    own_taps = [
        keep(taps.at[:, :cut], moved.at[0], tap_sems.at[0]),
        keep(taps.at[:, cut:], moved.at[1, :, : taps.shape[1] - cut], tap_sems.at[1]),
    ]

    place = lax.broadcasted_iota(jnp.int32, (64, pixels), 1) % 32

    def turn(i, part):
        at = slice(i * pixels, (i + 1) * pixels)
        for j in range(3):
            q = RATE_COLS[j]
            plain = part(j)
            value = plain.astype(f32)
            turned[j, :64, at] = jnp.where(place >= 32 - q, 0.0, pltpu.roll(value, pixels - q, 1)).astype(bf16)
            turned[j, 64:128, at] = plain
            turned[j, 128:, at] = jnp.where(place < q, 0.0, pltpu.roll(value, q, 1)).astype(bf16)

    pick = pick_rows(m, 64, group)
    turn(
        0,
        lambda j: lax.dot_general(
            pick, grads[:, j * m : (j + 1) * m], contract1, preferred_element_type=f32
        ).astype(bf16),
    )
    for copy in sent_picks:
        copy.wait()
    for k in (1, 2, 3):
        turn(k, lambda j: picked_in[k - 1, j * 64 : (j + 1) * 64])
    for copy in filled:
        copy.wait()
    for j in range(3):
        s = RATE_ROWS[j] * 32
        for a in range(3):
            if a == 1:
                low, high, start = 0, pixels, 64
            elif a == 0:
                low, high = s // 128 * 128, pixels
                start = 64 + low - s
            else:
                low, high, start = 0, -(-(pixels - s) // 128) * 128, 64 + s
            value = None
            for i in range(4):
                term = jnp.dot(
                    turned[j, :, i * pixels + low : i * pixels + high],
                    tpad[i, start : start + high - low],
                    preferred_element_type=f32,
                )
                value = term if value is None else value + term
            value = value.astype(bf16)
            for b in range(3):
                for to in range(2):
                    at = b * 64 + to * 32
                    zsend[to, (3 * j + a) * 3 + b] = value[at : at + 32]
    for name in ("valid", "norm3", "masked", "norm2", "norm1"):
        arrived[name].wait()

    def slopes(i, carry):
        at = rows(i * 32, 32)
        pre = norm3[at] * gain3[...] + bias3[...] + masked[at].astype(f32)
        gp3[at] = spread_lanes(valid[at], n) * slope(pre)
        gp2[at] = valid[at] * slope(norm2[at] * gain2[...] + bias2[...])
        slope1[at] = valid[at] * slope(norm1[at] * gain1[...] + bias1[...])
        return carry

    loop(pixels // 32, slopes, 0)
    zcopies = [keep(zsend.at[upper], aspp_parts.at[0], own_sems.at[2])]

    def send_parts(first, end):
        for i in range(first, end):
            zcopies.append(
                push(zsend.at[1 - upper, i], aspp_parts.at[1, i], z_sems.at[0, i], z_sems.at[1, i], (p ^ 4, c))
            )


    def over_z(blocks, sums, sems, own_sem):
        return [
            push(blocks.at[z ^ k], sums.at[z], sems.at[0, k], sems.at[1, k], (p ^ (2 * k), c)) for k in (3, 2, 1)
        ] + [keep(blocks.at[z], sums.at[z], own_sem)]

    def norm_back(grad, norm, sums, scale, gain, v):
        return gain * scale * (grad - v * (sums[0] + norm * sums[1]) / count)

    totals = []
    for h in range(2):
        for copy in back[h * PHASES : (h + 1) * PHASES]:
            copy.wait()
        if h == 1:
            send_parts(0, PACE[0])
        cols = slice(h * m, (h + 1) * m)

        def three(i, carry):
            at = rows(i * 64, 64)
            grad = drecv[h, at].astype(f32) * gp3[at, cols]
            gp3[at, cols] = grad
            return carry[0] + fold(grad), carry[1] + fold(grad * norm3[at, cols])

        zero = jnp.zeros((8, m), f32)
        bias, gain = loop(pixels // 64, three, (zero, zero))
        totals.append((total(bias), total(gain)))
    bias, gain = (jnp.concatenate([totals[0][i], totals[1][i]], axis=1) for i in range(2))
    packed_sums((bias, gain), st3)
    pix_exchange(st3, st3r, st_sems.at[0])
    send_parts(PACE[0], PACE[1])
    sums = unpacked_sums(st3r, n // 128, 2)
    sums_out[0:1] = sums[0]
    sums_out[1:2] = sums[1]

    arrived["expand"].wait()

    def part3(t):
        def step(i, carry):
            at = rows(t * tile + i * 32, 32)
            v = spread_lanes(valid[at], n)
            g3[at] = norm_back(gp3[at], norm3[at], sums, stats3[1:2], gain3[...], v).astype(bf16)
            return carry

        loop(tile // 32, step, 0)
        return lax.dot_general(g3[t * tile : (t + 1) * tile], expand[...], contract1, preferred_element_type=f32)

    result = sum_over_ch(part3, tile, TILES, own, out, near, cross, near_sems.at[0], far_sems.at[0])
    arrived["full2"].wait()
    value = lax.dot_general(full2[...], g3[...], contract0, preferred_element_type=f32).astype(bf16)
    for d in range(SPLIT):
        e_part[d] = value[d * mid : (d + 1) * mid]
    e_copies = [
        push(e_part.at[c ^ k], e_mid.at[c], ch_sems.at[0, 0, k], ch_sems.at[0, 1, k], (p, c ^ k)) for k in (2, 3, 1)
    ]
    e_copies.append(keep(e_part.at[c], e_mid.at[c], own_sems.at[3]))

    bias, gain = jnp.zeros((8, mid), f32), jnp.zeros((8, mid), f32)
    for t in range(TILES):
        hidden[t * tile : (t + 1) * tile] = result(t)

    def two(i, carry):
        at = rows(i * 128, 128)
        grad = hidden[at] * gp2[at]
        gp2[at] = grad
        return carry[0] + fold(grad), carry[1] + fold(grad * norm2[at])

    bias, gain = loop(pixels // 128, two, (bias, gain))
    packed_sums((total(bias), total(gain)), st2)
    pix_exchange(st2, st2r, st_sems.at[1])
    send_parts(PACE[1], PACE[2])
    for copy in e_copies:
        copy.wait()
    e_to_y = push(
        e_mid.at[:, :, rows((1 - y) * 256, 256)], e_in, pair_sems.at[0, 0], pair_sems.at[1, 0], (p ^ 1, c)
    )
    sums2 = unpacked_sums(st2r, 1, 2)
    sums_out[2:3, :mid] = sums2[0]
    sums_out[3:4, :mid] = sums2[1]

    def ready2(t):
        def step(i, carry):
            at = rows(t * tile + i * 128, 128)
            value = norm_back(gp2[at], norm2[at], sums2, stats2[1:2], gain2[...], valid[at])
            g2[at, rows(c * mid, mid)] = value.astype(bf16)
            return carry

        loop(tile // 128, step, 0)

    gather_over_ch(g2, mid, tile, TILES, gn, gf, gh, ready2)

    e_to_y.wait()
    for d in range(4):
        e_y[d] = (e_mid[d, :, rows(y * 256, 256)].astype(f32) + e_in[d].astype(f32)).astype(bf16)
    pix_copies = over_z(e_y, e_sum, pix_sems.at[0], own_sems.at[5])

    place = lax.broadcasted_iota(jnp.int32, (128, mid), 0) % 32

    def across(i, a):
        beta = i % COL_CLASSES
        two_on = (beta + 2) % 4 * 128
        here = slice(beta * 128, (beta + 1) * 128)
        there = slice(two_on, two_on + 128)
        lane = lambda b: slice((3 * a + b) * mid, (3 * a + b + 1) * mid)
        left, right = prod[there, lane(0)], prod[there, lane(2)]
        if beta >= 2:
            left = jnp.where(place == 31, 0.0, pltpu.roll(left, 127, 0))
        else:
            right = jnp.where(place == 0, 0.0, pltpu.roll(right, 1, 0))
        return prod[here, lane(1)] + left + right

    arrived["dilated"].wait()
    for i in range(PHASES):
        at = slice(i * 128, (i + 1) * 128)
        if i % COL_CLASSES == 0:
            prod[...] = lax.dot_general(
                g2[i * 128 : (i + COL_CLASSES) * 128], dilated[...], contract1, preferred_element_type=f32
            )
        up, same, down = across(i, 0), across(i, 1), across(i, 2)
        zero = jnp.zeros((32, mid), f32)
        hidden[at] = same + jnp.concatenate([up[32:], zero]) + jnp.concatenate([zero, down[:96]])
        edges[0, i] = up[:32].astype(bf16)
        edges[1, i] = down[96:].astype(bf16)
    first, last = p == 0, p == PHASES - 1
    to_next = lambda: pltpu.make_async_remote_copy(
        src_ref=edges.at[1], dst_ref=edges.at[2], send_sem=edge_sems.at[0, 0], recv_sem=edge_sems.at[1, 0],
        device_id=(p + 1, c), device_id_type=MESH,
    )
    to_last = lambda: pltpu.make_async_remote_copy(
        src_ref=edges.at[0], dst_ref=edges.at[3], send_sem=edge_sems.at[0, 1], recv_sem=edge_sems.at[1, 1],
        device_id=(p - 1, c), device_id_type=MESH,
    )

    @pl.when(jnp.logical_not(last))
    def _():
        to_next().start()

    @pl.when(jnp.logical_not(first))
    def _():
        to_last().start()

    @pl.when(first)
    def _():
        edges[2] = jnp.zeros((PHASES, 32, mid), bf16)

    @pl.when(last)
    def _():
        edges[3] = jnp.zeros((PHASES, 32, mid), bf16)

    for copy in own_taps:
        copy.wait()
    value = jnp.concatenate(
        [
            lax.dot_general(g2[...], moved[0], contract0, preferred_element_type=f32).astype(bf16),
            lax.dot_general(
                g2[...], moved[1, :, : taps.shape[1] - cut], contract0, preferred_element_type=f32
            ).astype(bf16),
        ],
        axis=1,
    )
    out_rows = SPLIT * mid // PHASES
    for d in range(PHASES):
        d_part[d % 2, d // 2] = value[d * out_rows : (d + 1) * out_rows]
    d_to_y = push(d_part.at[1 - y], d_in, pair_sems.at[0, 1], pair_sems.at[1, 1], (p ^ 1, c))

    @pl.when(jnp.logical_not(last))
    def _():
        to_next().wait_send()
        to_last().wait_recv()

    @pl.when(jnp.logical_not(first))
    def _():
        to_last().wait_send()
        to_next().wait_recv()

    send_parts(PACE[2], PACE[3])

    bias, gain = jnp.zeros((8, mid), f32), jnp.zeros((8, mid), f32)
    for i in range(PHASES):
        at = slice(i * 128, (i + 1) * 128)
        zero = jnp.zeros((64, mid), f32)
        edge = jnp.concatenate([edges[2, i].astype(f32), zero, edges[3, i].astype(f32)])
        grad = (hidden[at] + edge) * slope1[at]
        gp1[at] = grad
        bias, gain = bias + fold(grad), gain + fold(grad * norm1[at])
    packed_sums((total(bias), total(gain)), st1)
    pix_exchange(st1, st1r, st_sems.at[2])
    send_parts(PACE[3], 27)
    sums1 = unpacked_sums(st1r, 1, 2)
    sums_out[4:5, :mid] = sums1[0]
    sums_out[5:6, :mid] = sums1[1]

    def ready1(t):
        def step(i, carry):
            at = rows(t * tile + i * 128, 128)
            value = norm_back(gp1[at], norm1[at], sums1, stats1[1:2], gain1[...], valid[at])
            g1[at, rows(c * mid, mid)] = value.astype(bf16)
            return carry

        loop(tile // 128, step, 0)

    late = []

    def between():
        for copy in all_inputs:
            copy.wait()
        own_g1 = g1[:, rows(c * mid, mid)]
        for i in range(SPLIT):
            value = lax.dot_general(wide[2 * i, :, :n], own_g1[:n], contract0, preferred_element_type=f32)
            value = value + lax.dot_general(wide[2 * i + 1, :, :n], own_g1[n:], contract0, preferred_element_type=f32)
            r_mid[i] = value.astype(bf16).reshape(2, 256, mid)
        late.append(push(r_mid.at[:, 1 - y], r_in, pair_sems.at[0, 2], pair_sems.at[1, 2], (p ^ 1, c)))
        d_to_y.wait()
        for d in range(4):
            d_y[d // 2, d % 2] = (d_part[y, d].astype(f32) + d_in[d].astype(f32)).astype(bf16)
        late.append(push(d_y.at[:, 1 - lower], d_near, mid_sems.at[0, 0], mid_sems.at[1, 0], (p ^ 2, c)))

    gather_over_ch(g1, mid, tile, TILES, gn1, gf1, gh1, ready1, between)
    late[0].wait()
    for d in range(4):
        r_y[d] = (r_mid[d, y].astype(f32) + r_in[d].astype(f32)).astype(bf16)
    pix_copies += over_z(r_y, r_sum, pix_sems.at[2], own_sems.at[7])

    arrived["reduce"].wait()
    for i in range(PHASES):
        at = slice(i * 128, (i + 1) * 128)
        value = lax.dot_general(g1[at], reduce_rows[...], contract1, preferred_element_type=f32) + gp3[at]
        value = value * spread_lanes(valid[at], n)
        for g in range(n // 128):
            for r in range(4):
                start = (2 * r + i // COL_CLASSES) * 128 + i % COL_CLASSES
                lanes[g, pl.ds(start, 32, stride=COL_CLASSES), :] = value[r * 32 : (r + 1) * 32, g * 128 : (g + 1) * 128]
    for g in range(n // 128):
        features_grad[:, g * 128 : (g + 1) * 128] = lanes[g].astype(bf16)
    late[1].wait()
    for d in range(2):
        d_sum[d] = (d_y[d, lower].astype(f32) + d_near[d].astype(f32)).astype(bf16)
    d_last = push(d_sum.at[1 - upper], d_far, mid_sems.at[0, 1], mid_sems.at[1, 1], (p ^ 4, c))
    for copy in pix_copies:
        copy.wait()

    def gathered(parts):
        value = parts[0].astype(f32)
        for d in range(1, parts.shape[0]):
            value = value + parts[d].astype(f32)
        return value

    expand_grad[...] = gathered(e_sum)
    reduce_grad[...] = gathered(r_sum)
    d_last.wait()
    value = d_sum[upper].astype(f32) + d_far[...].astype(f32)
    for i in range(9):
        dilated_grad[i] = value[:, i * mid : (i + 1) * mid]
    for copy in zcopies:
        copy.wait()


def run_backward(cid, arrays):
    (grads, trunk, others, weight, norm3, masked, valid, expand, gain3, bias3, norm2, gain2, bias2, full2, taps, dilated,
     norm1, gain1, bias1, reduce_rows, stats1, stats2, stats3, picks, inputs) = arrays
    pixels, n = norm3.shape
    m = weight.shape[4]
    mid = norm2.shape[1]
    all_mid = SPLIT * mid
    outs = [
        shape((pixels, n), bf16),
        shape((2, 27, 32, n), bf16),
        shape((9, all_mid // PHASES, mid), f32),
        shape((mid, 256), f32),
        shape((256, mid), f32),
        shape((8, n), f32),
    ]
    sums = sum_scratch(pixels, mid, TILES)
    scratch = [
        pltpu.VMEM((9, n, 3 * m), bf16),
        pltpu.VMEM((3, pixels, 3 * m), bf16),
        pltpu.VMEM((pixels, m), f32),
        pltpu.VMEM((2, pixels, m), bf16),
        pltpu.VMEM((2, pixels, m), bf16),
        pltpu.VMEM((4, pixels + 128, n), bf16),
        pltpu.VMEM((4, 256, mid), bf16),
        pltpu.VMEM((3, 192, pixels), bf16),
        pltpu.VMEM((3, 192, 4 * pixels), bf16),
        pltpu.VMEM((2, 27, 32, n), bf16),
        pltpu.VMEM((4, 256, mid), bf16),
        pltpu.VMEM((pixels, n), f32),
        pltpu.VMEM((pixels, n), bf16),
        *sums[:4],
        pltpu.VMEM((pixels, mid), f32),
        pltpu.VMEM((pixels, mid), f32),
        pltpu.VMEM((pixels, all_mid), bf16),
        pltpu.VMEM((pixels // ROW_CLASSES, 9 * mid), f32),
        pltpu.VMEM((4, PHASES, 32, mid), bf16),
        pltpu.VMEM((pixels, all_mid), bf16),
        pltpu.VMEM((8, 128), f32),
        pltpu.VMEM((PHASES, 8, 128), f32),
        pltpu.VMEM((8, 128), f32),
        pltpu.VMEM((PHASES, 8, 128), f32),
        pltpu.VMEM((8, 128), f32),
        pltpu.VMEM((PHASES, 8, 128), f32),
        pltpu.VMEM((SPLIT, mid, n), bf16),
        pltpu.VMEM((SPLIT, mid, n), bf16),
        pltpu.VMEM((4, mid, 256), bf16),
        pltpu.VMEM((4, mid, 256), bf16),
        pltpu.VMEM((4, mid, 256), bf16),
        pltpu.VMEM((2, 4, all_mid // PHASES, 9 * mid), bf16),
        pltpu.VMEM((4, all_mid // PHASES, 9 * mid), bf16),
        pltpu.VMEM((2, 2, all_mid // PHASES, 9 * mid), bf16),
        pltpu.VMEM((2, all_mid // PHASES, 9 * mid), bf16),
        pltpu.VMEM((4, 2, 256, mid), bf16),
        pltpu.VMEM((4, 256, mid), bf16),
        dma(9, 3),
        dma(2, 2, PHASES),
        dma(3, 4),
        dma(2, 27),
        dma(1, 2, TILES, 2),
        dma(1, 2, TILES),
        dma(3, 2, PHASES),
        *gather_scratch(TILES),
        *gather_scratch(TILES),
        dma(2, 2),
        dma(2, 2, SPLIT),
        dma(3, 2, PHASES),
        dma(2, 3),
        dma(8),
        dma(2),
        dma(8),
        dma(4, 2, 2),
        dma(2, 2, 2),
        pltpu.VMEM((pixels, mid), f32),
        pltpu.VMEM((2, all_mid // PHASES, 9 * mid), bf16),
        pltpu.VMEM((all_mid // PHASES, 9 * mid), bf16),
        dma(2, 2),
        pltpu.VMEM((pixels, 128), f32),
        pltpu.VMEM((pixels, n), f32),
        pltpu.VMEM((pixels, n), bf16),
        pltpu.VMEM((all_mid, n), bf16),
        pltpu.VMEM((pixels, mid), f32),
        pltpu.VMEM((pixels, all_mid), bf16),
        pltpu.VMEM((pixels, mid), f32),
        pltpu.VMEM((9 * mid, all_mid), bf16),
        pltpu.VMEM((n, all_mid), bf16),
        dma(9),
    ]
    vmem = pl.BlockSpec(memory_space=pltpu.VMEM)
    specs = [vmem] * len(arrays)
    for i in (1, 2, 3, 4, 5, 6, 7, 10, 13, 14, 15, 16, 19, 24):
        specs[i] = pl.BlockSpec(memory_space=pl.ANY)
    return pl.pallas_call(
        backward,
        out_shape=outs,
        in_specs=specs,
        out_specs=[vmem, pl.BlockSpec(memory_space=pl.ANY)] + [vmem] * (len(outs) - 2),
        scratch_shapes=scratch,
        compiler_params=pltpu.CompilerParams(
            collective_id=cid, has_side_effects=True, vmem_limit_bytes=VMEM_BYTES
        ),
        name="backward",
    )(*arrays)


def fast_device(
    features,
    pixel_mask,
    reduce_weight,
    reduce_gain,
    reduce_bias,
    dilated_weight,
    dilated_gain,
    dilated_bias,
    expand_weight,
    expand_gain,
    expand_bias,
    aspp_weight,
    aspp_gain,
    aspp_bias,
    task_weight,
    cotangent,
):
    rows_here, width, local_in = features.shape
    pixels = rows_here * width
    local_mid = reduce_weight.shape[1]
    full_mid = dilated_weight.shape[3]
    branch_width = aspp_weight.shape[4]
    own_branch = task_weight.shape[1]
    outs_count = task_weight.shape[2]
    me_ch = lax.axis_index("ch")
    line = lambda v: v.reshape(1, -1)
    dilated_rows = dilated_weight.reshape(9 * local_mid, full_mid)
    (
        masked, reduce_rows, expand_cols, norm_one, valid, norm_two, act_two_full, taps_one, norm_three, trunk_class,
        stat_one, stat_two, stat_three, inputs_all, grad_full, predictions, head_grad, branch_sums, trunk_others, picks,
    ) = run_forward(
        1,
        features.reshape(pixels, local_in),
        pixel_mask,
        reduce_weight,
        expand_weight,
        line(reduce_gain),
        line(reduce_bias),
        task_weight.transpose(0, 2, 1),
        aspp_gain,
        aspp_bias,
        cotangent.transpose(2, 0, 1).reshape(outs_count, pixels),
        dilated_rows,
        line(dilated_gain),
        line(dilated_bias),
        line(expand_gain),
        line(expand_bias),
        aspp_weight,
    )
    features_grad, aspp_parts, dilated_sum, expand_weight_grad, reduce_weight_grad, norm_sums = run_backward(
        2,
        [
            grad_full, trunk_class, trunk_others, aspp_weight, norm_three, masked, valid, expand_cols,
            line(expand_gain), line(expand_bias), norm_two, line(dilated_gain), line(dilated_bias), act_two_full,
            taps_one, dilated_rows, norm_one, line(reduce_gain), line(reduce_bias), reduce_rows, stat_one, stat_two,
            stat_three, picks, inputs_all,
        ],
    )
    features_grad = features_grad.reshape(rows_here, width, local_in)
    aspp_weight_grad = (aspp_parts[0].astype(f32) + aspp_parts[1].astype(f32)).reshape(
        3, 3, 3, -1, local_in
    ).transpose(0, 1, 2, 4, 3)
    dilated_weight_grad = dilated_sum.reshape(3, 3, -1, local_mid).transpose(0, 1, 3, 2)
    expand_bias_grad, expand_gain_grad = norm_sums[0], norm_sums[1]
    dilated_bias_grad, dilated_gain_grad = norm_sums[2, :local_mid], norm_sums[3, :local_mid]
    reduce_bias_grad, reduce_gain_grad = norm_sums[4, :local_mid], norm_sums[5, :local_mid]
    predictions = from_classes(predictions.transpose(0, 2, 1), rows_here, width)[:, :, :outs_count]
    head_grad = head_grad.reshape(32, 3, 4, own_branch).transpose(2, 1, 3, 0)
    task_weight_grad = lax.dynamic_index_in_dim(head_grad, me_ch, keepdims=False)[:, :, :outs_count]
    own_sums = lax.dynamic_slice_in_dim(
        branch_sums[:6].reshape(2, 3, branch_width), me_ch * own_branch, own_branch, axis=2
    )
    aspp_bias_grad, aspp_gain_grad = own_sums[0], own_sums[1]

    return (
        predictions,
        features_grad,
        reduce_weight_grad,
        reduce_gain_grad,
        reduce_bias_grad,
        dilated_weight_grad,
        dilated_gain_grad,
        dilated_bias_grad,
        expand_weight_grad,
        expand_gain_grad,
        expand_bias_grad,
        aspp_weight_grad,
        aspp_gain_grad,
        aspp_bias_grad,
        task_weight_grad,
    )


def solution(mesh):
    placed = (
        P("pix", None, "ch"),
        P("pix", None),
        P(None, "ch"),
        P("ch"),
        P("ch"),
        P(None, None, "ch", None),
        P("ch"),
        P("ch"),
        P("ch", None),
        P("ch"),
        P("ch"),
        P(None, None, None, "ch", None),
        P(None, "ch"),
        P(None, "ch"),
        P(None, "ch", None),
        P("pix", None, None),
    )
    return jax.shard_map(
        fast_device if (mesh.shape["pix"], mesh.shape["ch"]) == (PHASES, 4) else on_device,
        mesh=mesh,
        in_specs=placed,
        out_specs=(
            P("pix", None, None),
            P("pix", None, "ch"),
            P("pix", "ch"),
            P("ch"),
            P("ch"),
            P(None, None, "ch", "pix"),
            P("ch"),
            P("ch"),
            P("ch", "pix"),
            P("ch"),
            P("ch"),
            P(None, None, None, "ch", "pix"),
            P(None, "ch"),
            P(None, "ch"),
            P(None, "ch", None),
        ),
        check_vma=False,
    )
```

profile of v0, /device:TPU:0, one launch (start us, length us, event | category | flops | bytes accessed | tf_op | source)
XLA Modules:
  0.0 266.9 jit_solution(1229203269396827566)
XLA Ops:
  0.6 0.9 pad
  1.5 0.7 copy.37
  2.2 138.7 %forward.1 = (bf16[1024,512]{1,0:T(8,128)(2,1)}, bf16[512,512]{1,0:T(8,128)(2,1)}, bf16[512,512]{1,0:T(8,128)(2,1)}, f32[1024,128]{1,0:T(8,128)}, f32[1024,128]{...) custom-call(bf16[1024,512]{1,0:T(8,128)(2,1)} %bitcast.51, ...), custom_call_target="tpu_custom_call" | custom-call | tf_op jit(solution)/shard_map/forward/pallas_call | solution.py:341
  141.0 0.7 reshape.100
  141.7 0.7 dynamic-slice_bitcast_fusion
  142.3 1.0 reshape.101
  143.4 0.6 slice.53
  144.0 1.2 reshape.96
  145.2 0.3 copy.33
  145.5 0.8 copy.35
  146.3 111.4 %backward.1 = (bf16[1024,512]{1,0:T(8,128)(2,1)}, bf16[2,27,32,512]{3,2,1,0:T(8,128)(2,1)}, f32[9,64,128]{2,1,0:T(8,128)}, f32[128,256]{1,0:T(8,128)}, f32[256,128]{1,0:T(8,128)}, /*index=5*/f32[8,512]{1,0:T(8,128)}) custom-call(bf16[1024,768]{1,0:T(8,128)(2,1)} %get-tuple-element.42.grads, bf16[2,1024,256]{2,1,0:T(8,128)(2,1)} %get-tuple-element.43.trunk, ...), custom_call_target="tpu_custom_call" | custom-call | tf_op jit(solution)/shard_map/backward/pallas_call | solution.py:1867
  257.7 1.3 slice_bitcast_fusion
  259.0 1.4 fusion
  260.4 0.0 copy-start
  260.4 3.1 %convert_add_fusion = f32[1,27,32,512]{3,2,1,0:T(8,128)} fusion(bf16[2,27,32,512]{3,2,1,0:T(8,128)(2,1)} %get-tuple-element.64), kind=kLoop, calls=%fused_computation | loop fusion | flops 1327104 | bytes 3538944 | tf_op jit(solution)/shard_map/add | solution.py:1940
  263.4 0.0 copy-start.3
  263.4 0.0 copy-start.1
  263.5 0.0 copy-start.2
  263.5 0.0 copy-done
  263.5 1.0 copy.44
  264.4 0.0 copy-done.3
  264.4 0.7 copy.45
  265.1 0.0 copy-done.1
  265.1 0.7 copy.46
  265.8 0.0 copy-done.2
  265.8 0.7 copy.47
  (2 shorter events, 0.1 us)
Async XLA Ops:
  260.4 3.1 %copy-start = (bf16[1024,512]{1,0:T(8,128)(2,1)S(1)}, bf16[1024,512]{1,0:T(8,128)(2,1)}, u32[]{:S(2)}) copy-start(bf16[1024,512]{1,0:T(8,128)(2,1)} %get-tuple-element.59) | copy-start | bytes 3145732
  263.4 1.0 copy-start.3
  263.4 1.6 copy-start.1
  263.5 2.4 copy-start.2
where the time goes:
time: 272 us; the launch traced here: 267 us
  Pallas kernels  250 us (92%)
  local copies, waits for them, and re-layouts  12.6 us (5%)
  other arithmetic  3.05 us (1%)
    pallas_call x1, Pallas kernels, call(): pl.pallas_call(kernel, out_shape=outs, in_specs=[hbm if i in hbm_ins else...  139 us
    pallas_call x1, Pallas kernels, run_backward(): pl.pallas_call(backward, out_shape=outs, in_specs=specs, out_specs=[vmem,...  111 us

commit v1 on v0

--- a/solution.py
+++ b/solution.py
@@ -327,7 +327,7 @@
 ROW_CLASSES, COL_CLASSES = 2, 4
 PHASES = ROW_CLASSES * COL_CLASSES
 SPLIT = 4
-FAR_FIRST = (6, 7, 4, 5, 2, 3, 1)
+FAR_FIRST = (1, 2, 3, 4, 5, 6, 7)
 f32, bf16 = jnp.float32, jnp.bfloat16
 VMEM_BYTES = 60 << 20
 
@@ -463,7 +463,7 @@
         copy.wait()
 
 
-def norm_stats(hidden, valid, pixels, send, recv, sems):
+def norm_stats(hidden, valid, pixels, send, recv, sems, counted=None):
     n = hidden.shape[1]
     tile = 128
     repeat = n // 128
@@ -488,6 +488,21 @@
         return carry + fold(mask(at) * apart * apart)
 
     spread = total(loop(pixels // tile, second, zero))
+    if counted is not None:
+        groups = n // 128
+        for i in range(groups):
+            send[i : i + 1] = sums[:, i * 128 : (i + 1) * 128]
+            send[groups + i : groups + i + 1] = spread[:, i * 128 : (i + 1) * 128]
+        pix_exchange(send, recv, sems)
+        sums = [
+            jnp.concatenate([recv[d, i : i + 1] for i in range(groups)], axis=1) for d in range(PHASES)
+        ]
+        spreads = [
+            jnp.concatenate([recv[d, groups + i : groups + i + 1] for i in range(groups)], axis=1)
+            for d in range(PHASES)
+        ]
+        counts = [spread_lanes(counted[d, 2:3], n) for d in range(PHASES)]
+        return join_parts(sums, spreads, counts)
     send[0:1] = sums
     send[1:2] = spread
     send[2:3] = count
@@ -495,17 +510,24 @@
     return join(recv, PHASES)
 
 
+def spread_lanes(v, n):
+    return v if n == 128 else jnp.concatenate([v] * (n // 128), axis=1)
+
+
+def join_parts(sums, spreads, counts):
+    whole, count = sums[0], counts[0]
+    for i in range(1, len(sums)):
+        whole, count = whole + sums[i], count + counts[i]
+    center = whole / count
+    spread = jnp.zeros_like(whole)
+    for i in range(len(sums)):
+        apart = sums[i] / jnp.maximum(counts[i], 1.0) - center
+        spread = spread + spreads[i] + counts[i] * apart * apart
+    return center, lax.rsqrt(spread / count + epsilon), count
+
+
 def join(recv, parts):
-    sums, count = recv[0, 0:1], recv[0, 2:3]
-    for i in range(1, parts):
-        sums, count = sums + recv[i, 0:1], count + recv[i, 2:3]
-    center = sums / count
-    spread = jnp.zeros_like(sums)
-    for i in range(parts):
-        n = recv[i, 2:3]
-        apart = recv[i, 0:1] / jnp.maximum(n, 1.0) - center
-        spread = spread + recv[i, 1:2] + n * apart * apart
-    return center, lax.rsqrt(spread / count + epsilon), count
+    return join_parts(*[[recv[i, row : row + 1] for i in range(parts)] for row in range(3)])
 
 
 def stat_scratch(n):
@@ -1115,7 +1137,7 @@
     gather_over_ch(full, local_mid, tile, TILES, g_near, g_far, g_hop, ready)
 
 
-def stage_three(full, weight, masked, valid, gain, bias, *refs):
+def stage_three(full, weight, masked, valid, gain, bias, counted, *refs):
     (norm, classes, stat, inputs) = refs[:4]
     (hidden, trunk, send, recv, stat_sems, class_sems, own_sem, in_sems) = refs[4:]
     p, c = lax.axis_index("pix"), lax.axis_index("ch")
@@ -1127,7 +1149,7 @@
     far = push(masked, inputs.at[c], in_sems.at[0, 0], in_sems.at[1, 0], (p, c ^ 2))
     near = push(masked, inputs.at[c], in_sems.at[0, 1], in_sems.at[1, 1], (p, c ^ 1))
     mine = keep(masked, inputs.at[c], own_sem.at[2])
-    center, scale, count = norm_stats(hidden, valid, pixels, send, recv, stat_sems)
+    center, scale, count = norm_stats(hidden, valid, pixels, send, recv, stat_sems, counted)
     stat[0:1] = center
     stat[1:2] = scale
     stat[2:3] = count
@@ -1204,6 +1226,7 @@
     expand_copies = stage_one(
         feat, mask, weight, expand, gain1, bias1, masked, reduce_rows, expand_cols, norm1, padded, stat1, valid, *own[:one]
     )
+    counted = own[9]
     own = own[one:]
     save(0, 1, 3, 4)
     stage_two(padded, valid, dilated, gain2, bias2, norm2, full2, taps, stat2, *own[:two])
@@ -1212,7 +1235,7 @@
         copy.wait()
     save(2, 5, 6, 7)
     moving, pass_inputs = stage_three(
-        full2, expand_cols, masked, valid, gain3, bias3, norm3, classes, stat3, inputs, *own[:three]
+        full2, expand_cols, masked, valid, gain3, bias3, counted, norm3, classes, stat3, inputs, *own[:three]
     )
     own = own[three:]
     save(8)
@@ -1279,7 +1302,7 @@
         *gather_scratch(TILES),
         pltpu.VMEM((pixels, n), f32),
         pltpu.VMEM((2, pixels, n // 2), bf16),
-        *stat_scratch(n),
+        *stat_scratch(128),
         dma(2, 2, PHASES),
         dma(4),
         dma(2, 3),
@@ -1325,10 +1348,6 @@
             i += 1
         out.append(parts[0] if rows_each == 1 else jnp.concatenate(parts, axis=1))
     return out
-
-
-def spread_lanes(v, n):
-    return v if n == 128 else jnp.concatenate([v] * (n // 128), axis=1)
 
 
 def backward(
@@ -1877,6 +1896,81 @@
     )(*arrays)
 
 
+def publish(features, parts, dilated, expand, reduce, norm_sums, predictions, head_grad, branch_sums, *outs):
+    (o_predictions, o_features, o_reduce, o_gain1, o_bias1, o_dilated, o_gain2, o_bias2, o_expand, o_gain3, o_bias3,
+     o_parts, o_branch_gain, o_branch_bias, o_heads) = outs
+    c = lax.axis_index("ch")
+    columns, mid = o_predictions.shape[0], o_gain1.shape[1]
+    m = o_heads.shape[2]
+    o_features[...] = features[...]
+    o_reduce[...] = reduce[...]
+    o_expand[...] = expand[...]
+    o_dilated[...] = dilated[...]
+    for i in range(parts.shape[1]):
+        o_parts[i] = parts[0, i].astype(f32) + parts[1, i].astype(f32)
+    o_bias3[...] = norm_sums[0:1]
+    o_gain3[...] = norm_sums[1:2]
+    o_bias2[...] = norm_sums[2:3, :mid]
+    o_gain2[...] = norm_sums[3:4, :mid]
+    o_bias1[...] = norm_sums[4:5, :mid]
+    o_gain1[...] = norm_sums[5:6, :mid]
+
+    def own(value):
+        return jnp.where(lax.rem(c, 2) == 1, value[:, m:], value[:, :m])
+
+    lanes = rows(c // 2 * 2 * m, 2 * m)
+    value = own(branch_sums[:, lanes])
+    o_branch_bias[...] = value[0:3]
+    o_branch_gain[...] = value[3:6]
+    for j in range(3):
+        value = own(head_grad[:, rows(j * SPLIT * m + c // 2 * 2 * m, 2 * m)])
+        o_heads[j] = value[:columns]
+    place = jnp.where(
+        one_hot(512, 512, lambda i: i % 128 // 32 * 128 + 4 * (i % 32) + i // 128), 1.0, 0.0
+    ).astype(bf16)
+    for a in range(ROW_CLASSES):
+        value = jnp.concatenate([predictions[a * COL_CLASSES + b] for b in range(COL_CLASSES)], axis=1)
+        high = value.astype(bf16)
+        rest = value - high.astype(f32)
+        middle = rest.astype(bf16)
+        low = (rest - middle.astype(f32)).astype(bf16)
+        value = jnp.dot(jnp.concatenate([high, middle, low]), place, preferred_element_type=f32)
+        value = value[:32] + (value[32:64] + value[64:])
+        for r in range(4):
+            o_predictions[:, 2 * r + a, :] = value[:columns, r * 128 : (r + 1) * 128]
+
+
+def run_publish(columns, m, arrays):
+    features, parts, dilated, expand, reduce = arrays[:5]
+    n, mid = features.shape[1], reduce.shape[1]
+    outs = [
+        shape((columns, 8, 128), f32),
+        shape(features.shape, bf16),
+        shape(reduce.shape, f32),
+        shape((1, mid), f32),
+        shape((1, mid), f32),
+        shape(dilated.shape, f32),
+        shape((1, mid), f32),
+        shape((1, mid), f32),
+        shape(expand.shape, f32),
+        shape((1, n), f32),
+        shape((1, n), f32),
+        shape(parts.shape[1:], f32),
+        shape((3, m), f32),
+        shape((3, m), f32),
+        shape((3, columns, m), f32),
+    ]
+    vmem = pl.BlockSpec(memory_space=pltpu.VMEM)
+    return pl.pallas_call(
+        publish,
+        out_shape=outs,
+        in_specs=[vmem] * len(arrays),
+        out_specs=[vmem] * len(outs),
+        compiler_params=pltpu.CompilerParams(vmem_limit_bytes=VMEM_BYTES),
+        name="publish",
+    )(*arrays)
+
+
 def fast_device(
     features,
     pixel_mask,
@@ -1902,7 +1996,6 @@
     branch_width = aspp_weight.shape[4]
     own_branch = task_weight.shape[1]
     outs_count = task_weight.shape[2]
-    me_ch = lax.axis_index("ch")
     line = lambda v: v.reshape(1, -1)
     dilated_rows = dilated_weight.reshape(9 * local_mid, full_mid)
     (
@@ -1936,38 +2029,34 @@
             stat_three, picks, inputs_all,
         ],
     )
-    features_grad = features_grad.reshape(rows_here, width, local_in)
-    aspp_weight_grad = (aspp_parts[0].astype(f32) + aspp_parts[1].astype(f32)).reshape(
-        3, 3, 3, -1, local_in
-    ).transpose(0, 1, 2, 4, 3)
-    dilated_weight_grad = dilated_sum.reshape(3, 3, -1, local_mid).transpose(0, 1, 3, 2)
-    expand_bias_grad, expand_gain_grad = norm_sums[0], norm_sums[1]
-    dilated_bias_grad, dilated_gain_grad = norm_sums[2, :local_mid], norm_sums[3, :local_mid]
-    reduce_bias_grad, reduce_gain_grad = norm_sums[4, :local_mid], norm_sums[5, :local_mid]
-    predictions = from_classes(predictions.transpose(0, 2, 1), rows_here, width)[:, :, :outs_count]
-    head_grad = head_grad.reshape(32, 3, 4, own_branch).transpose(2, 1, 3, 0)
-    task_weight_grad = lax.dynamic_index_in_dim(head_grad, me_ch, keepdims=False)[:, :, :outs_count]
-    own_sums = lax.dynamic_slice_in_dim(
-        branch_sums[:6].reshape(2, 3, branch_width), me_ch * own_branch, own_branch, axis=2
-    )
-    aspp_bias_grad, aspp_gain_grad = own_sums[0], own_sums[1]
-
+    (
+        predictions, features_grad, reduce_weight_grad, reduce_gain_grad, reduce_bias_grad, dilated_weight_grad,
+        dilated_gain_grad, dilated_bias_grad, expand_weight_grad, expand_gain_grad, expand_bias_grad, aspp_weight_grad,
+        aspp_gain_grad, aspp_bias_grad, task_weight_grad,
+    ) = run_publish(
+        outs_count,
+        own_branch,
+        [
+            features_grad, aspp_parts, dilated_sum, expand_weight_grad, reduce_weight_grad, norm_sums, predictions,
+            head_grad, branch_sums,
+        ],
+    )
     return (
-        predictions,
-        features_grad,
+        predictions.transpose(1, 2, 0),
+        features_grad.reshape(rows_here, width, local_in),
         reduce_weight_grad,
-        reduce_gain_grad,
-        reduce_bias_grad,
-        dilated_weight_grad,
-        dilated_gain_grad,
-        dilated_bias_grad,
+        reduce_gain_grad.reshape(-1),
+        reduce_bias_grad.reshape(-1),
+        dilated_weight_grad.reshape(3, 3, -1, local_mid).transpose(0, 1, 3, 2),
+        dilated_gain_grad.reshape(-1),
+        dilated_bias_grad.reshape(-1),
         expand_weight_grad,
-        expand_gain_grad,
-        expand_bias_grad,
-        aspp_weight_grad,
+        expand_gain_grad.reshape(-1),
+        expand_bias_grad.reshape(-1),
+        aspp_weight_grad.reshape(3, 3, 3, -1, local_in).transpose(0, 1, 2, 4, 3),
         aspp_gain_grad,
         aspp_bias_grad,
-        task_weight_grad,
+        task_weight_grad.transpose(0, 2, 1),
     )
 
 

time: 272 us -> 261 us (0.960)
  local copies, waits for them, and re-layouts: 12.6 us -> 1.56 us
  Pallas kernels: 250 us -> 254 us
  other arithmetic: 3.05 us -> 0 us
    pallas_call x0 -> x1, Pallas kernels: none -> 4.24 us  [run_publish(): pl.pallas_call(publish, out_shape=outs, in_specs=[vmem] * len(arrays), ou...]
    unnamed x16 -> x2, local copies, waits for them, and re-layouts: 5.41 us -> 1.56 us
    reshape x4 -> x0, local copies, waits for them, and re-layouts: 3.14 us -> none  [the longest x2 1.42 us: from_classes(): x.reshape(ROW_CLASSES, COL_CLASSES, rows // ROW_CLASSES, cols // COL_CLAS...]
    add x1 -> x0, other arithmetic: 3.05 us -> none  [fast_device(): aspp_parts[0].astype(f32) + aspp_parts[1].astype(f32)]
where the time goes in v1:
time: 261 us; the launch traced here: 256 us
  Pallas kernels  254 us (97%)
    pallas_call x1, Pallas kernels, call(): pl.pallas_call(kernel, out_shape=outs, in_specs=[hbm if i in hbm_ins else...  138 us
    pallas_call x1, Pallas kernels, run_backward(): pl.pallas_call(backward, out_shape=outs, in_specs=specs, out_specs=[vmem,...  112 us

profile of v1, /device:TPU:0, one launch (start us, length us, event | category | flops | bytes accessed | tf_op | source)
XLA Modules:
  0.0 256.5 jit_solution(2956612044001617123)
XLA Ops:
  0.6 0.9 pad
  1.5 0.7 copy.31
  2.2 138.0 %forward.1 = (bf16[1024,512]{1,0:T(8,128)(2,1)}, bf16[512,512]{1,0:T(8,128)(2,1)}, bf16[512,512]{1,0:T(8,128)(2,1)}, f32[1024,128]{1,0:T(8,128)}, f32[1024,128]{...) custom-call(bf16[1024,512]{1,0:T(8,128)(2,1)} %bitcast.30, ...), custom_call_target="tpu_custom_call" | custom-call | tf_op jit(solution)/shard_map/forward/pallas_call | solution.py:341
  140.3 111.5 %backward.1 = (bf16[1024,512]{1,0:T(8,128)(2,1)}, bf16[2,27,32,512]{3,2,1,0:T(8,128)(2,1)}, f32[9,64,128]{2,1,0:T(8,128)}, f32[128,256]{1,0:T(8,128)}, f32[256,128]{1,0:T(8,128)}, /*index=5*/f32[8,512]{1,0:T(8,128)}) custom-call(bf16[1024,768]{1,0:T(8,128)(2,1)} %get-tuple-element.56.grads, bf16[2,1024,256]{2,1,0:T(8,128)(2,1)} %get-tuple-element.57.trunk, ...), custom_call_target="tpu_custom_call" | custom-call | tf_op jit(solution)/shard_map/backward/pallas_call | solution.py:1886
  251.8 4.2 %publish.1 = (f32[23,8,128]{2,1,0:T(8,128)}, bf16[1024,512]{1,0:T(8,128)(2,1)}, f32[256,128]{1,0:T(8,128)}, f32[1,128]{1,0:T(1,128)}, f32[1,128]{1,0:T(1,128)}, ...) custom-call(bf16[1024,512]{1,0:T(8,128)(2,1)} %get-tuple-element.73., ...), custom_call_target="tpu_custom_call" | custom-call | tf_op jit(solution)/shard_map/publish/pallas_call | solution.py:1964

commit v2 on v1

--- a/solution.py
+++ b/solution.py
@@ -1325,7 +1325,7 @@
     return call("forward", cid, forward, arrays, outs, scratch, hbm_ins=(15,), hbm_outs=(*range(10), 13, 18))
 
 
-PACE = (1, 10, 18, 21)
+PACE = (1, 10, 20, 23)
 
 
 def packed_sums(values, send):
@@ -1698,7 +1698,30 @@
     out_rows = SPLIT * mid // PHASES
     for d in range(PHASES):
         d_part[d % 2, d // 2] = value[d * out_rows : (d + 1) * out_rows]
-    d_to_y = push(d_part.at[1 - y], d_in, pair_sems.at[0, 1], pair_sems.at[1, 1], (p ^ 1, c))
+    halves = [pl.ds(h * out_rows // 2, out_rows // 2) for h in range(2)]
+    d_to_y = [
+        push(d_part.at[1 - y, :, at], d_in.at[:, at], mid_sems.at[0, 4 + h], mid_sems.at[1, 4 + h], (p ^ 1, c))
+        for h, at in enumerate(halves)
+    ]
+    d_to_z, d_across = [], []
+
+    def add_y(h):
+        at = halves[h]
+        d_to_y[h].wait()
+        for d in range(4):
+            d_y[d // 2, d % 2, at] = (d_part[y, d, at].astype(f32) + d_in[d, at].astype(f32)).astype(bf16)
+        d_to_z.append(
+            push(d_y.at[:, 1 - lower, at], d_near.at[:, at], mid_sems.at[0, h], mid_sems.at[1, h], (p ^ 2, c))
+        )
+
+    def add_z(h):
+        at = halves[h]
+        d_to_z[h].wait()
+        for d in range(2):
+            d_sum[d, at] = (d_y[d, lower, at].astype(f32) + d_near[d, at].astype(f32)).astype(bf16)
+        d_across.append(
+            push(d_sum.at[1 - upper, at], d_far.at[at], mid_sems.at[0, 2 + h], mid_sems.at[1, 2 + h], (p ^ 4, c))
+        )
 
     @pl.when(jnp.logical_not(last))
     def _():
@@ -1722,6 +1745,7 @@
         bias, gain = bias + fold(grad), gain + fold(grad * norm1[at])
     packed_sums((total(bias), total(gain)), st1)
     pix_exchange(st1, st1r, st_sems.at[2])
+    add_y(0)
     send_parts(PACE[3], 27)
     sums1 = unpacked_sums(st1r, 1, 2)
     sums_out[4:5, :mid] = sums1[0]
@@ -1747,16 +1771,15 @@
             value = value + lax.dot_general(wide[2 * i + 1, :, :n], own_g1[n:], contract0, preferred_element_type=f32)
             r_mid[i] = value.astype(bf16).reshape(2, 256, mid)
         late.append(push(r_mid.at[:, 1 - y], r_in, pair_sems.at[0, 2], pair_sems.at[1, 2], (p ^ 1, c)))
-        d_to_y.wait()
-        for d in range(4):
-            d_y[d // 2, d % 2] = (d_part[y, d].astype(f32) + d_in[d].astype(f32)).astype(bf16)
-        late.append(push(d_y.at[:, 1 - lower], d_near, mid_sems.at[0, 0], mid_sems.at[1, 0], (p ^ 2, c)))
+        add_y(1)
+        add_z(0)
 
     gather_over_ch(g1, mid, tile, TILES, gn1, gf1, gh1, ready1, between)
     late[0].wait()
     for d in range(4):
         r_y[d] = (r_mid[d, y].astype(f32) + r_in[d].astype(f32)).astype(bf16)
     pix_copies += over_z(r_y, r_sum, pix_sems.at[2], own_sems.at[7])
+    add_z(1)
 
     arrived["reduce"].wait()
     for i in range(PHASES):
@@ -1769,10 +1792,6 @@
                 lanes[g, pl.ds(start, 32, stride=COL_CLASSES), :] = value[r * 32 : (r + 1) * 32, g * 128 : (g + 1) * 128]
     for g in range(n // 128):
         features_grad[:, g * 128 : (g + 1) * 128] = lanes[g].astype(bf16)
-    late[1].wait()
-    for d in range(2):
-        d_sum[d] = (d_y[d, lower].astype(f32) + d_near[d].astype(f32)).astype(bf16)
-    d_last = push(d_sum.at[1 - upper], d_far, mid_sems.at[0, 1], mid_sems.at[1, 1], (p ^ 4, c))
     for copy in pix_copies:
         copy.wait()
 
@@ -1784,7 +1803,8 @@
 
     expand_grad[...] = gathered(e_sum)
     reduce_grad[...] = gathered(r_sum)
-    d_last.wait()
+    for copy in d_across:
+        copy.wait()
     value = d_sum[upper].astype(f32) + d_far[...].astype(f32)
     for i in range(9):
         dilated_grad[i] = value[:, i * mid : (i + 1) * mid]
@@ -1867,7 +1887,7 @@
         pltpu.VMEM((pixels, mid), f32),
         pltpu.VMEM((2, all_mid // PHASES, 9 * mid), bf16),
         pltpu.VMEM((all_mid // PHASES, 9 * mid), bf16),
-        dma(2, 2),
+        dma(2, 6),
         pltpu.VMEM((pixels, 128), f32),
         pltpu.VMEM((pixels, n), f32),
         pltpu.VMEM((pixels, n), bf16),

time: 261 us -> 260 us (level)
  no operation moved by 1% of the time
where the time goes in v2:
time: 260 us; the launch traced here: 255 us
  Pallas kernels  252 us (97%)
    pallas_call x1, Pallas kernels, call(): pl.pallas_call(kernel, out_shape=outs, in_specs=[hbm if i in hbm_ins else...  138 us
    pallas_call x1, Pallas kernels, run_backward(): pl.pallas_call(backward, out_shape=outs, in_specs=specs, out_specs=[vmem,...  110 us

profile of v2, /device:TPU:0, one launch (start us, length us, event | category | flops | bytes accessed | tf_op | source)
XLA Modules:
  0.0 255.0 jit_solution(14461788138932540151)
XLA Ops:
  0.6 0.9 pad
  1.5 0.7 copy.31
  2.2 138.0 %forward.1 = (bf16[1024,512]{1,0:T(8,128)(2,1)}, bf16[512,512]{1,0:T(8,128)(2,1)}, bf16[512,512]{1,0:T(8,128)(2,1)}, f32[1024,128]{1,0:T(8,128)}, f32[1024,128]{...) custom-call(bf16[1024,512]{1,0:T(8,128)(2,1)} %bitcast.30, ...), custom_call_target="tpu_custom_call" | custom-call | tf_op jit(solution)/shard_map/forward/pallas_call | solution.py:341
  140.3 110.1 %backward.1 = (bf16[1024,512]{1,0:T(8,128)(2,1)}, bf16[2,27,32,512]{3,2,1,0:T(8,128)(2,1)}, f32[9,64,128]{2,1,0:T(8,128)}, f32[128,256]{1,0:T(8,128)}, f32[256,128]{1,0:T(8,128)}, /*index=5*/f32[8,512]{1,0:T(8,128)}) custom-call(bf16[1024,768]{1,0:T(8,128)(2,1)} %get-tuple-element.56.grads, bf16[2,1024,256]{2,1,0:T(8,128)(2,1)} %get-tuple-element.57.trunk, ...), custom_call_target="tpu_custom_call" | custom-call | tf_op jit(solution)/shard_map/backward/pallas_call | solution.py:1906
  250.3 4.2 %publish.1 = (f32[23,8,128]{2,1,0:T(8,128)}, bf16[1024,512]{1,0:T(8,128)(2,1)}, f32[256,128]{1,0:T(8,128)}, f32[1,128]{1,0:T(1,128)}, f32[1,128]{1,0:T(1,128)}, ...) custom-call(bf16[1024,512]{1,0:T(8,128)(2,1)} %get-tuple-element.73., ...), custom_call_target="tpu_custom_call" | custom-call | tf_op jit(solution)/shard_map/publish/pallas_call | solution.py:1984

commit v3 on v2

--- a/solution.py
+++ b/solution.py
@@ -1062,7 +1062,7 @@
     image[...] = jnp.zeros(image.shape, f32)
     for r in range(8):
         at = slice(r * 128, (r + 1) * 128)
-        image[:columns, at] = cotangent[:, at] * present[r : r + 1]
+        image[:columns, at] = cotangent[:, r, :] * present[r : r + 1]
         image[31:32, at] = present[r : r + 1]
     square[...] = jnp.zeros(square.shape, f32)
     square[:, :32] = lax.dot_general(
@@ -2032,7 +2032,7 @@
         task_weight.transpose(0, 2, 1),
         aspp_gain,
         aspp_bias,
-        cotangent.transpose(2, 0, 1).reshape(outs_count, pixels),
+        cotangent.transpose(2, 0, 1),
         dilated_rows,
         line(dilated_gain),
         line(dilated_bias),

time: 260 us -> 258 us (level)
  no operation moved by 1% of the time
where the time goes in v3:
time: 258 us; the launch traced here: 254 us
  Pallas kernels  252 us (98%)
    pallas_call x1, Pallas kernels, call(): pl.pallas_call(kernel, out_shape=outs, in_specs=[hbm if i in hbm_ins else...  138 us
    pallas_call x1, Pallas kernels, run_backward(): pl.pallas_call(backward, out_shape=outs, in_specs=specs, out_specs=[vmem,...  110 us

profile of v3, /device:TPU:0, one launch (start us, length us, event | category | flops | bytes accessed | tf_op | source)
XLA Modules:
  0.0 253.5 jit_solution(6824403262850620885)
XLA Ops:
  0.6 138.1 %forward.1 = (bf16[1024,512]{1,0:T(8,128)(2,1)}, bf16[512,512]{1,0:T(8,128)(2,1)}, bf16[512,512]{1,0:T(8,128)(2,1)}, f32[1024,128]{1,0:T(8,128)}, f32[1024,128]{...) custom-call(bf16[1024,512]{1,0:T(8,128)(2,1)} %bitcast.27, ...), custom_call_target="tpu_custom_call" | custom-call | tf_op jit(solution)/shard_map/forward/pallas_call | solution.py:341
  138.8 110.1 %backward.1 = (bf16[1024,512]{1,0:T(8,128)(2,1)}, bf16[2,27,32,512]{3,2,1,0:T(8,128)(2,1)}, f32[9,64,128]{2,1,0:T(8,128)}, f32[128,256]{1,0:T(8,128)}, f32[256,128]{1,0:T(8,128)}, /*index=5*/f32[8,512]{1,0:T(8,128)}) custom-call(bf16[1024,768]{1,0:T(8,128)(2,1)} %get-tuple-element.56.grads, bf16[2,1024,256]{2,1,0:T(8,128)(2,1)} %get-tuple-element.57.trunk, ...), custom_call_target="tpu_custom_call" | custom-call | tf_op jit(solution)/shard_map/backward/pallas_call | solution.py:1906
  248.8 4.2 %publish.1 = (f32[23,8,128]{2,1,0:T(8,128)}, bf16[1024,512]{1,0:T(8,128)(2,1)}, f32[256,128]{1,0:T(8,128)}, f32[1,128]{1,0:T(1,128)}, f32[1,128]{1,0:T(1,128)}, ...) custom-call(bf16[1024,512]{1,0:T(8,128)(2,1)} %get-tuple-element.73., ...), custom_call_target="tpu_custom_call" | custom-call | tf_op jit(solution)/shard_map/publish/pallas_call | solution.py:1984
